TPU v7x, 32 devices: a whole 2x2x4 slice. The times are simulated.
32 devices in a mesh: head: 2 (over core), blk: 16 (over z, y, x).
Axes of the slice: x: 2, y: 2, z: 4, core: 2. Of those that a mesh axis runs over, the one named last changes fastest.
Arguments:
- inputs: bfloat16 [16, 1024, 768], P('blk', 'head'), may hold values from -6 to 6
- positions: int32 [16, 1024], P('blk', 'head'), may hold values from 0 to 15359, as said below
- w_query: bfloat16 [768, 768], P(('head', 'blk')), may hold values from -0.21875 to 0.21875
- w_key: bfloat16 [768, 768], P(('head', 'blk')), may hold values from -0.21875 to 0.21875
- w_value: bfloat16 [768, 768], P(('head', 'blk')), may hold values from -0.21875 to 0.21875
- w_out: bfloat16 [768, 768], P(('head', 'blk')), may hold values from -1.5 to 1.5
- w_up: bfloat16 [768, 3072], P(('head', 'blk')), may hold values from -0.21875 to 0.21875
- bias_up: bfloat16 [3072], P(('head', 'blk')), may hold values from -3 to 3
- w_down: bfloat16 [3072, 768], P(('head', 'blk')), may hold values from -0.109375 to 0.109375
- bias_down: bfloat16 [768], P(('head', 'blk')), may hold values from -3 to 3
- gain_mid: bfloat16 [768], P(('head', 'blk')), may hold values from 0.5 to 1.5
- shift_mid: bfloat16 [768], P(('head', 'blk')), may hold values from -3 to 3
- gain_out: bfloat16 [768], P(('head', 'blk')), may hold values from 0.5 to 1.5
- shift_out: bfloat16 [768], P(('head', 'blk')), may hold values from -3 to 3
- grad_out: bfloat16 [16, 1024, 768], P('blk', 'head'), may hold values from -6 to 6
Outputs:
- output: bfloat16 [16, 1024, 768], P('blk', 'head')
- grad_inputs: float32 [16, 1024, 768], P('blk', 'head')
- grad_w_query: float32 [768, 768], P(('head', 'blk'))
- grad_w_key: float32 [768, 768], P(('head', 'blk'))
- grad_w_value: float32 [768, 768], P(('head', 'blk'))
- grad_w_out: float32 [768, 768], P(('head', 'blk'))
- grad_w_up: float32 [768, 3072], P(('head', 'blk'))
- grad_bias_up: float32 [3072], P(('head', 'blk'))
- grad_w_down: float32 [3072, 768], P(('head', 'blk'))
- grad_bias_down: float32 [768], P(('head', 'blk'))
- grad_gain_mid: float32 [768], P(('head', 'blk'))
- grad_shift_mid: float32 [768], P(('head', 'blk'))
- grad_gain_out: float32 [768], P(('head', 'blk'))
- grad_shift_out: float32 [768], P(('head', 'blk'))
Inputs may be any that keep to these rules, and one draw needn't show every extreme that they name: `positions`: positions count 0, 1, 2, ... from each document's first token. One document begins inside the first segment and is 15360 tokens long, so that it ends inside the last segment; shorter documents fill the stream before and after it.
All inputs are finite; a program needn't handle non-finite values.
Results may differ from a plain program's by a relative error of at most 0.017.
Values may be sent and summed in bfloat16 or wider, within the bound.
A program may use at most 192 MiB of HBM per device.

v0:
```python
import jax
import jax.numpy as jnp
from jax import lax
from jax.sharding import PartitionSpec as P

HEADS = 12
HEAD_DIM = 64
SUB = 512


eps = 1e-05
half_pi = 1.5707963267948966
highest = lax.Precision.HIGHEST


def prefix(array, axis, join, neutral, backward):
    count = lax.axis_size(axis)
    place = lax.axis_index(axis)
    ahead = count - 1 - place if backward else place
    gathered = jax.tree.map(
        lambda a, kind: lax.all_gather(a.astype(kind), axis),
        array,
        jax.tree.map(lambda a: jnp.bfloat16 if a.dtype == jnp.float32 else a.dtype, array),
    )
    state = jax.tree.map(lambda a, e: jnp.zeros_like(a) + jnp.asarray(e, a.dtype), array, neutral)

    def one(step, state):
        source = count - 1 - step if backward else step
        return join(
            state,
            jax.tree.map(
                lambda a, own: lax.dynamic_index_in_dim(a, source, 0, False).astype(own.dtype),
                gathered,
                array,
            ),
        )

    return lax.fori_loop(0, ahead, one, state)


def block_tail(block_positions):
    width_now = block_positions.shape[-1]
    places = jnp.arange(width_now, dtype=jnp.int32)
    last_position = block_positions[..., width_now - 1 :]
    tail_mask = (width_now - 1 - places <= last_position).astype(jnp.float32)
    keeping = (last_position >= width_now).astype(jnp.float32)
    return (tail_mask, keeping)


def block_masks(block_positions):
    width_now = block_positions.shape[-1]
    places = jnp.arange(width_now, dtype=jnp.int32)
    causal = (
        (places[None, :] <= places[:, None])
        & (places[:, None] - places[None, :] <= block_positions[:, None])
    ).astype(jnp.float32)
    use_mask = (block_positions > places).astype(jnp.float32)
    return (causal, use_mask)


def chain_link(earlier, following):
    factor = following[2]
    return (
        factor * earlier[0] + following[0],
        factor[..., 0] * earlier[1] + following[1],
        earlier[2] * following[2],
    )


def norm_rows(values, gain_factor, shift_term):
    centered = values - jnp.mean(values, axis=-1, keepdims=True)
    inv_scale = lax.rsqrt(jnp.mean(centered * centered, axis=-1, keepdims=True) + eps)
    normed = centered * inv_scale
    return (normed * gain_factor + shift_term, normed, inv_scale)


def norm_back(grad_rows, normed, inv_scale, gain_factor):
    grad_norm = grad_rows * gain_factor
    inner_term = (
        grad_norm
        - jnp.mean(grad_norm, axis=-1, keepdims=True)
        - normed * jnp.mean(grad_norm * normed, axis=-1, keepdims=True)
    )
    return (inv_scale * inner_term, jnp.sum(grad_rows * normed, axis=0), jnp.sum(grad_rows, axis=0))


def features(raw_rows, cosine, sine_wave):
    soft_part = jax.nn.softplus(raw_rows.astype(jnp.float32))
    return jnp.concatenate([soft_part * cosine, soft_part * sine_wave], axis=-1).astype(
        jnp.bfloat16
    )


def block_forward(query_features, key_features, values, block_positions, state_in, total_in):
    causal, use_mask = block_masks(block_positions)
    scores = (
        jnp.einsum("ihf,jhf->hij", query_features, key_features, preferred_element_type=jnp.float32)
        * causal[None]
    )
    weights = scores.astype(jnp.bfloat16)
    query_wide = query_features.astype(jnp.float32)
    numerator = jnp.einsum("hij,jhd->ihd", weights, values, preferred_element_type=jnp.float32)
    numerator = numerator + use_mask[:, None, None] * jnp.einsum(
        "ihf,hfd->ihd", query_wide, state_in, precision=highest
    )
    denominator = jnp.sum(weights, axis=2, dtype=jnp.float32).T + use_mask[:, None] * jnp.einsum(
        "ihf,hf->ih", query_wide, total_in, precision=highest
    )
    return (numerator / denominator[:, :, None], weights, denominator, causal, use_mask)


def block_backward(
    query_features, key_features, values, block_positions, state_in, total_in, grad_mixed
):
    mixed_rows, weights, denominator, causal, use_mask = block_forward(
        query_features, key_features, values, block_positions, state_in, total_in
    )
    grad_wide = grad_mixed.astype(jnp.float32)
    grad_numer = (grad_wide / denominator[:, :, None]).astype(jnp.bfloat16)
    grad_denom = -jnp.sum(grad_wide * mixed_rows, axis=2) / denominator
    grad_scores = (
        jnp.einsum("ihd,jhd->hij", grad_numer, values, preferred_element_type=jnp.float32)
        + grad_denom.T[:, :, None]
    )
    grad_scores = (grad_scores * causal[None]).astype(jnp.bfloat16)
    query_wide = query_features.astype(jnp.float32)
    numer_wide = grad_numer.astype(jnp.float32)
    grad_queries = jnp.einsum(
        "hij,jhf->ihf", grad_scores, key_features, preferred_element_type=jnp.float32
    )
    grad_queries = grad_queries + use_mask[:, None, None] * (
        jnp.einsum("ihd,hfd->ihf", numer_wide, state_in, precision=highest)
        + grad_denom[:, :, None] * total_in[None]
    )
    grad_keys = jnp.einsum(
        "hij,ihf->jhf", grad_scores, query_features, preferred_element_type=jnp.float32
    )
    grad_values = jnp.einsum(
        "hij,ihd->jhd", weights, grad_numer, preferred_element_type=jnp.float32
    )
    used_queries = query_wide * use_mask[:, None, None]
    use_state = jnp.einsum("ihf,ihd->hfd", used_queries, numer_wide, precision=highest)
    use_total = jnp.einsum("ihf,ih->hf", used_queries, grad_denom, precision=highest)
    return (grad_queries, grad_keys, grad_values, use_state, use_total)


def local(
    inputs,
    positions,
    w_query,
    w_key,
    w_value,
    w_out,
    w_up,
    bias_up,
    w_down,
    bias_down,
    gain_mid,
    shift_mid,
    gain_out,
    shift_out,
    grad_out,
):
    head_split = lax.axis_size("head")
    cycle_size = lax.axis_size("blk")
    token_rows = inputs.shape[1]
    segment_rows = token_rows * head_split
    local_heads = HEADS // head_split
    local_width = local_heads * HEAD_DIM
    feature_width = 2 * HEAD_DIM
    blocks = segment_rows // SUB
    reach_tokens = float(segment_rows * cycle_size)
    tokens = inputs[0]
    gathered = (
        lax.all_gather(w_query, ("head", "blk"), axis=0, tiled=True),
        lax.all_gather(w_key, ("head", "blk"), axis=0, tiled=True),
        lax.all_gather(w_value, ("head", "blk"), axis=0, tiled=True),
        lax.all_gather(w_out, ("head", "blk"), axis=0, tiled=True),
        lax.all_gather(w_up, ("head", "blk"), axis=0, tiled=True),
        lax.all_gather(bias_up, ("head", "blk"), axis=0, tiled=True),
        lax.all_gather(w_down, ("head", "blk"), axis=0, tiled=True),
        lax.all_gather(bias_down, ("head", "blk"), axis=0, tiled=True),
        lax.all_gather(gain_mid, ("head", "blk"), axis=0, tiled=True),
        lax.all_gather(shift_mid, ("head", "blk"), axis=0, tiled=True),
        lax.all_gather(gain_out, ("head", "blk"), axis=0, tiled=True),
        lax.all_gather(shift_out, ("head", "blk"), axis=0, tiled=True),
    )
    (
        query_full,
        key_full,
        value_full,
        out_full,
        up_full,
        lift_bias,
        down_full,
        drop_bias,
        mid_gain,
        mid_shift,
        end_gain,
        end_shift,
    ) = gathered
    queries = jnp.dot(tokens, query_full, preferred_element_type=jnp.float32).astype(jnp.bfloat16)
    key_rows = jnp.dot(tokens, key_full, preferred_element_type=jnp.float32).astype(jnp.bfloat16)
    value_rows = jnp.dot(tokens, value_full, preferred_element_type=jnp.float32).astype(
        jnp.bfloat16
    )
    spread = (
        lax.all_to_all(queries, "head", split_axis=1, concat_axis=0, tiled=True),
        lax.all_to_all(key_rows, "head", split_axis=1, concat_axis=0, tiled=True),
        lax.all_to_all(value_rows, "head", split_axis=1, concat_axis=0, tiled=True),
    )
    segment_positions = lax.all_gather(positions, "head", axis=1, tiled=True)[0]
    angles = segment_positions.astype(jnp.float32) * (half_pi / reach_tokens)
    cosine = jnp.cos(angles)[:, None, None]
    sine_wave = jnp.sin(angles)[:, None, None]
    head_queries = spread[0].reshape(segment_rows, local_heads, HEAD_DIM)
    head_keys = spread[1].reshape(segment_rows, local_heads, HEAD_DIM)
    query_features = features(head_queries, cosine, sine_wave).reshape(
        blocks, SUB, local_heads, feature_width
    )
    key_features = features(head_keys, cosine, sine_wave).reshape(
        blocks, SUB, local_heads, feature_width
    )
    value_blocks = spread[2].reshape(blocks, SUB, local_heads, HEAD_DIM)
    position_blocks = segment_positions.reshape(blocks, SUB)
    tails, keeps = block_tail(position_blocks)
    weighted = key_features * tails[:, :, None, None].astype(jnp.bfloat16)
    add_state = jnp.einsum(
        "bjhf,bjhd->bhfd", weighted, value_blocks, preferred_element_type=jnp.float32
    )
    add_total = jnp.sum(weighted, axis=1, dtype=jnp.float32)
    keep_list = [keeps[number].reshape(1, 1, 1) for number in range(blocks)]
    summary = (add_state[0], add_total[0], keep_list[0])
    number = 1
    summary = chain_link(summary, (add_state[number], add_total[number], keep_list[number]))
    identity = (
        jnp.zeros_like(add_state[0]),
        jnp.zeros_like(add_total[0]),
        jnp.ones((1, 1, 1), jnp.float32),
    )
    entering = prefix(summary, "blk", chain_link, identity, False)
    carry_state = entering[0]
    carry_total = entering[1]
    states = []
    totals = []
    for number in range(blocks):
        states.append(carry_state)
        totals.append(carry_total)
        carry_state = keep_list[number] * carry_state + add_state[number]
        carry_total = keep_list[number][..., 0] * carry_total + add_total[number]
    state_stack = jnp.stack(states)
    total_stack = jnp.stack(totals)
    mixed_blocks = lax.map(
        lambda block_data: block_forward(*block_data)[0],
        (query_features, key_features, value_blocks, position_blocks, state_stack, total_stack),
    )
    mixed_local = mixed_blocks.reshape(segment_rows, local_width).astype(jnp.bfloat16)
    mixed_tokens = lax.all_to_all(mixed_local, "head", split_axis=0, concat_axis=1, tiled=True)
    attended = jnp.dot(mixed_tokens, out_full, preferred_element_type=jnp.float32)
    middle = tokens.astype(jnp.float32) + attended
    mid_rows, normed_mid, scale_mid = norm_rows(
        middle, mid_gain.astype(jnp.float32), mid_shift.astype(jnp.float32)
    )
    mid_rounded = mid_rows.astype(jnp.bfloat16)
    up_rows = jnp.dot(mid_rounded, up_full, preferred_element_type=jnp.float32) + lift_bias.astype(
        jnp.float32
    )
    gelu_rows, gelu_back = jax.vjp(jax.nn.gelu, up_rows)
    active = gelu_rows.astype(jnp.bfloat16)
    after_ffn = (
        mid_rows
        + jnp.dot(active, down_full, preferred_element_type=jnp.float32)
        + drop_bias.astype(jnp.float32)
    )
    result, normed_end, scale_end = norm_rows(
        after_ffn, end_gain.astype(jnp.float32), end_shift.astype(jnp.float32)
    )
    output = result.astype(jnp.bfloat16)[None]
    (
        query_back,
        key_back,
        value_back,
        out_back,
        up_back,
        lift_back,
        down_back,
        drop_back,
        mid_gain_back,
        mid_shift_back,
        end_gain_back,
        end_shift_back,
    ) = gathered
    grad_rows = grad_out[0].astype(jnp.float32)
    grad_after, grad_end_gain, grad_end_shift = norm_back(
        grad_rows, normed_end, scale_end, end_gain_back.astype(jnp.float32)
    )
    grad_branch = grad_after.astype(jnp.bfloat16)
    grad_down = jnp.einsum("tf,td->fd", active, grad_branch, preferred_element_type=jnp.float32)
    grad_drop = jnp.sum(grad_branch, axis=0, dtype=jnp.float32)
    grad_active = jnp.einsum(
        "td,fd->tf", grad_branch, down_back, preferred_element_type=jnp.float32
    )
    grad_lift_rows = gelu_back(grad_active)[0].astype(jnp.bfloat16)
    grad_up = jnp.einsum(
        "td,tf->df", mid_rounded, grad_lift_rows, preferred_element_type=jnp.float32
    )
    grad_lift = jnp.sum(grad_lift_rows, axis=0, dtype=jnp.float32)
    grad_mid_rows = (
        jnp.einsum("tf,df->td", grad_lift_rows, up_back, preferred_element_type=jnp.float32)
        + grad_after
    )
    grad_middle, grad_mid_gain, grad_mid_shift = norm_back(
        grad_mid_rows, normed_mid, scale_mid, mid_gain_back.astype(jnp.float32)
    )
    grad_attn = grad_middle.astype(jnp.bfloat16)
    grad_out_weight = jnp.einsum(
        "tc,td->cd", mixed_tokens, grad_attn, preferred_element_type=jnp.float32
    )
    grad_mixed = jnp.einsum(
        "td,cd->tc", grad_attn, out_back, preferred_element_type=jnp.float32
    ).astype(jnp.bfloat16)
    grad_heads = lax.all_to_all(grad_mixed, "head", split_axis=1, concat_axis=0, tiled=True)
    grad_blocks = grad_heads.reshape(blocks, SUB, local_heads, HEAD_DIM)
    backward_parts = lax.map(
        lambda block_data: block_backward(*block_data),
        (
            query_features,
            key_features,
            value_blocks,
            position_blocks,
            state_stack,
            total_stack,
            grad_blocks,
        ),
    )
    grad_qf, grad_kf, grad_vf, use_state, use_total = backward_parts
    local_state = jnp.zeros_like(add_state[0])
    local_total = jnp.zeros_like(add_total[0])
    for number in reversed(range(blocks)):
        local_state = use_state[number] + keep_list[number] * local_state
        local_total = use_total[number] + keep_list[number][..., 0] * local_total
    beyond = prefix((local_state, local_total, summary[2]), "blk", chain_link, identity, True)
    later_state = beyond[0]
    later_total = beyond[1]
    grad_adds = [None] * blocks
    grad_adds_total = [None] * blocks
    for number in reversed(range(blocks)):
        grad_adds[number] = later_state
        grad_adds_total[number] = later_total
        later_state = use_state[number] + keep_list[number] * later_state
        later_total = use_total[number] + keep_list[number][..., 0] * later_total
    grad_add_state = jnp.stack(grad_adds)
    grad_add_total = jnp.stack(grad_adds_total)
    tail_wide = tails[:, :, None, None]
    value_wide = value_blocks.astype(jnp.float32)
    key_wide = key_features.astype(jnp.float32)
    grad_kf = grad_kf + tail_wide * (
        jnp.einsum("bjhd,bhfd->bjhf", value_wide, grad_add_state, precision=highest)
        + grad_add_total[:, None]
    )
    grad_vf = grad_vf + tail_wide * jnp.einsum(
        "bjhf,bhfd->bjhd", key_wide, grad_add_state, precision=highest
    )

    def feature_back(grad_feature, raw_rows):
        grad_feature = grad_feature.reshape(segment_rows, local_heads, feature_width)
        grad_soft = grad_feature[..., :HEAD_DIM] * cosine + grad_feature[..., HEAD_DIM:] * sine_wave
        return (
            (grad_soft * jax.nn.sigmoid(raw_rows.astype(jnp.float32)))
            .astype(jnp.bfloat16)
            .reshape(segment_rows, local_width)
        )

    grad_query_rows = feature_back(grad_qf, head_queries)
    grad_key_rows = feature_back(grad_kf, head_keys)
    grad_value_rows = grad_vf.reshape(segment_rows, local_width).astype(jnp.bfloat16)
    returned = (
        lax.all_to_all(grad_query_rows, "head", split_axis=0, concat_axis=1, tiled=True),
        lax.all_to_all(grad_key_rows, "head", split_axis=0, concat_axis=1, tiled=True),
        lax.all_to_all(grad_value_rows, "head", split_axis=0, concat_axis=1, tiled=True),
    )
    grad_query = jnp.einsum("tc,td->cd", tokens, returned[0], preferred_element_type=jnp.float32)
    grad_key = jnp.einsum("tc,td->cd", tokens, returned[1], preferred_element_type=jnp.float32)
    grad_value = jnp.einsum("tc,td->cd", tokens, returned[2], preferred_element_type=jnp.float32)
    grad_inputs = grad_middle + jnp.einsum(
        "td,cd->tc", returned[0], query_back, preferred_element_type=jnp.float32
    )
    grad_inputs = grad_inputs + jnp.einsum(
        "td,cd->tc", returned[1], key_back, preferred_element_type=jnp.float32
    )
    grad_inputs = grad_inputs + jnp.einsum(
        "td,cd->tc", returned[2], value_back, preferred_element_type=jnp.float32
    )
    summed = tuple(
        (
            lax.psum_scatter(grad_query, ("head", "blk"), scatter_dimension=0, tiled=True),
            lax.psum_scatter(grad_key, ("head", "blk"), scatter_dimension=0, tiled=True),
            lax.psum_scatter(grad_value, ("head", "blk"), scatter_dimension=0, tiled=True),
            lax.psum_scatter(grad_out_weight, ("head", "blk"), scatter_dimension=0, tiled=True),
            lax.psum_scatter(grad_up, ("head", "blk"), scatter_dimension=0, tiled=True),
            lax.psum_scatter(grad_lift, ("head", "blk"), scatter_dimension=0, tiled=True),
            lax.psum_scatter(grad_down, ("head", "blk"), scatter_dimension=0, tiled=True),
            lax.psum_scatter(grad_drop, ("head", "blk"), scatter_dimension=0, tiled=True),
            lax.psum_scatter(grad_mid_gain, ("head", "blk"), scatter_dimension=0, tiled=True),
            lax.psum_scatter(grad_mid_shift, ("head", "blk"), scatter_dimension=0, tiled=True),
            lax.psum_scatter(grad_end_gain, ("head", "blk"), scatter_dimension=0, tiled=True),
            lax.psum_scatter(grad_end_shift, ("head", "blk"), scatter_dimension=0, tiled=True),
        )
    )
    return (output, grad_inputs[None]) + summed


def solution(mesh):
    in_specs = (
        P("blk", "head", None),
        P("blk", "head"),
        P(("head", "blk"), None),
        P(("head", "blk"), None),
        P(("head", "blk"), None),
        P(("head", "blk"), None),
        P(("head", "blk"), None),
        P(("head", "blk")),
        P(("head", "blk"), None),
        P(("head", "blk")),
        P(("head", "blk")),
        P(("head", "blk")),
        P(("head", "blk")),
        P(("head", "blk")),
        P("blk", "head", None),
    )
    out_specs = (
        P("blk", "head", None),
        P("blk", "head", None),
        P(("head", "blk"), None),
        P(("head", "blk"), None),
        P(("head", "blk"), None),
        P(("head", "blk"), None),
        P(("head", "blk"), None),
        P(("head", "blk")),
        P(("head", "blk"), None),
        P(("head", "blk")),
        P(("head", "blk")),
        P(("head", "blk")),
        P(("head", "blk")),
        P(("head", "blk")),
    )
    return jax.shard_map(local, mesh=mesh, in_specs=in_specs, out_specs=out_specs, check_vma=False)
```

profile of v0, /device:TPU:0, one launch (start us, length us, event | category | flops | bytes accessed | tf_op | source)
XLA Modules:
  0.0 1271.9 jit_solution(5215106460803580750)
XLA Ops:
  14.2 53.5 %all-gather.12.cloned.1.call-done = bf16[768,768]{1,0:T(8,128)(2,1)} async-done(((bf16[24,768]{1,0:T(8,128)(2,1)}), bf16[768,768]{1,0:T(8,128)(2,1)}) %all-gather.12.cloned.1.call-update) | async-done | bytes 1179664 | tf_op jit(solution)/shard_map/all_gather | solution.py:175
  70.3 4.4 all_to_all.128
  77.1 46.5 %all-gather.14.cloned.1.call-done = bf16[768,768]{1,0:T(8,128)(2,1)} async-done(((bf16[24,768]{1,0:T(8,128)(2,1)}), bf16[768,768]{1,0:T(8,128)(2,1)}) %all-gather.14.cloned.1.call-update) | async-done | bytes 1179664 | tf_op jit(solution)/shard_map/all_gather | solution.py:176
  126.0 4.4 all_to_all.129
  132.8 46.7 %all-gather.10.cloned.1.call-done = bf16[768,768]{1,0:T(8,128)(2,1)} async-done(((bf16[24,768]{1,0:T(8,128)(2,1)}), bf16[768,768]{1,0:T(8,128)(2,1)}) %all-gather.10.cloned.1.call-update) | async-done | bytes 1179664 | tf_op jit(solution)/shard_map/all_gather | solution.py:177
  181.7 4.4 all_to_all.130
  186.4 7.5 multiply_convert_fusion.7
  203.2 39.8 %all-reduce = bf16[16]{0:T(256)(128)(2,1)S(1)} all-reduce(bf16[16]{0:T(256)(128)(2,1)S(1)} %dynamic-update-slice), channel_id=2, replica_groups=mesh['head'=2,'blk'=16] {'blk'}, use_global_device_ids=true, to_apply=%add | all-reduce | flops 16 | bytes 64
  244.4 37.2 %all-reduce.14 = (bf16[768]{0:T(1024)(128)(2,1)S(1)}, bf16[768]{0:T(1024)(128)(2,1)S(1)}, bf16[768]{0:T(1024)(128)(2,1)S(1)}, bf16[3072]{0:T(1024)(128)(2,1)S(1)...) all-reduce(bf16[768]{0:T(1024)(128)(2,1)S(1)} %dynamic-update-slice, ...), channel_id=1, replica_groups=mesh['head'=2,'blk'=16] {'head','blk'}, use_global_device_ids=true, to_apply=%add.4 | all-reduce | flops 6912 | bytes 27648
  285.9 39.5 %all_gather.70 = bf16[16,6,128]{2,1,0:T(8,128)(2,1)S(1)} all-gather(bf16[1,6,128]{2,1,0:T(8,128)(2,1)S(1)} %fusion.126), channel_id=1, replica_groups=mesh['head'=2,'blk'=16] {'blk'}, dimensions={0}, use_global_device_ids=true | all-gather | bytes 26112 | tf_op jit(solution)/shard_map/all_gather | solution.py:21
  333.2 8.8 while.63
  342.0 4.3 all-to-all-start.3
  352.5 23.7 %all-gather.20.cloned.1.call-done = bf16[768,3072]{1,0:T(8,128)(2,1)} async-done(((bf16[24,3072]{1,0:T(8,128)(2,1)}), bf16[768,3072]{1,0:T(8,128)(2,1)}) %all-gather.20.cloned.1.call-update) | async-done | bytes 4718608 | tf_op jit(solution)/shard_map/all_gather | solution.py:179
  376.2 8.2 fusion.144
  384.4 57.2 %all-gather.22.cloned.1.call-done = bf16[3072,768]{1,0:T(8,128)(2,1)} async-done(((bf16[96,768]{1,0:T(8,128)(2,1)}), bf16[3072,768]{1,0:T(8,128)(2,1)}) %all-gather.22.cloned.1.call-update) | async-done | bytes 4718608 | tf_op jit(solution)/shard_map/all_gather | solution.py:181
  441.6 8.9 fusion.151
  455.2 7.1 convert_reduce_fusion.2
  462.3 3.7 multiply_reduce_fusion
  468.5 5.5 all_to_all.131
  476.3 30.6 %while.64 = (s32[]{:T(128)}, f32[2,512,6,128]{3,1,0,2:T(8,128)}, f32[2,512,6,128]{1,3,2,0:T(8,128)}, f32[2,512,6,64]{1,3,2,0:T(8,128)}, f32[2,6,128,64]{2,3,1,0:...) while((s32[]{:T(128)}, f32[2,512,6,128]{3,1,0,2:T(8,128)}, ...), condition=%wide.region_17.18_spmd.clone, body=%wide.region_14.17_spmd.sunk.clone | while | flops 2746371072 | bytes 111482840 | solution.py:324
  509.6 38.7 %all_gather.81 = bf16[16,6,128]{2,1,0:T(8,128)(2,1)S(1)} all-gather(bf16[1,6,128]{2,1,0:T(8,128)(2,1)S(1)} %add_convert_fusion.2), channel_id=1, replica_groups=mesh['head'=2,'blk'=16] {'blk'}, dimensions={0}, use_global_device_ids=true | all-gather | bytes 26112 | tf_op jit(solution)/shard_map/all_gather | solution.py:21
  548.3 4.1 fusion.120
  552.5 12.6 all-gather.24.cloned.1.call-done
  565.1 38.5 %while.65 = (s32[]{:T(128)}, f32[6,128,64]{2,1,0:T(8,128)S(1)}, f32[6,128]{1,0:T(8,128)S(1)}, s32[]{:T(128)}, bf16[16,1,1,1]{0,3,2,1:T(2,128)(2,1)S(1)}, /*index...) while((s32[]{:T(128)}, f32[6,128,64]{2,1,0:T(8,128)S(1)}, ...), condition=%wide.region_19.20_spmd.clone, body=%wide.region_18.19_spmd.sunk.clone | while | flops 149767 | bytes 892569 | solution.py:38
  604.4 3.2 fusion.108
  607.6 4.5 all_to_all.132
  614.3 3.2 copy.265
  621.5 3.5 reshape.395
  627.8 3.4 reshape.397
  631.2 6.5 fusion.147
  637.7 3.2 copy.271
  640.9 3.3 copy.272
  644.9 5.2 bitcast_add_fusion.1
  650.1 3.5 copy.235
  653.7 6.4 fusion.148
  660.1 3.2 copy.273
  663.3 3.2 copy.274
  666.6 5.0 multiply_convert_fusion.9
  674.2 4.5 all_to_all.133
  685.6 4.4 all_to_all.134
  696.7 7.3 fusion.142
  705.4 10.3 fusion.135
  716.9 37.6 %all-reduce.13 = (f32[3072]{0:T(1024)S(1)}, f32[768]{0:T(1024)S(1)}, f32[768]{0:T(1024)S(1)}, f32[768]{0:T(1024)S(1)}, f32[768]{0:T(1024)S(1)}, /*index=5*/f32[768]{0:T(1024)S(1)}) all-reduce(f32[3072]{0:T(1024)S(1)} %copy-done.48, f32[768]{0:T(1024)S(1)} %copy-done.45, ...), channel_id=8, replica_groups=mesh['head'=2,'blk'=16] {'head','blk'}, use_global_device_ids=true, to_apply=%region_26.27.clone | all-reduce | flops 6912 | bytes 55296
  764.1 9.3 reduce-scatter.23.cloned.1.call-done
  773.4 104.1 %reduce-scatter.19.cloned.1.call-done = f32[24,768]{1,0:T(8,128)} async-done(((f32[768,768]{1,0:T(8,128)}), f32[24,768]{1,0:T(8,128)}) %reduce-scatter.19.cloned.1.call-update) | async-done | bytes 73744
  877.4 104.6 %reduce-scatter.21.cloned.1.call-done = f32[24,768]{1,0:T(8,128)} async-done(((f32[768,768]{1,0:T(8,128)}), f32[24,768]{1,0:T(8,128)}) %reduce-scatter.21.cloned.1.call-update) | async-done | bytes 73744
  982.0 141.2 %reduce-scatter.15.cloned.1.call-done = f32[24,3072]{1,0:T(8,128)} async-done(((f32[768,3072]{1,0:T(8,128)}), f32[24,3072]{1,0:T(8,128)}) %reduce-scatter.15.cloned.1.call-update) | async-done | bytes 294928 | tf_op jit(solution)/shard_map/reduce_scatter | solution.py:400
  1123.2 142.0 %reduce-scatter.17.cloned.1.call-done = f32[96,768]{1,0:T(8,128)} async-done(((f32[3072,768]{1,0:T(8,128)}), f32[96,768]{1,0:T(8,128)}) %reduce-scatter.17.cloned.1.call-update) | async-done | bytes 294928 | tf_op jit(solution)/shard_map/reduce_scatter | solution.py:402
  (441 shorter events, 163.4 us)
Async XLA Ops:
  7.2 60.5 %all-gather.12.cloned.1.call-start = ((), (), s32[]{:S(2)}) async-start(), calls=%async_computation.15 | async-start | bytes 1216512 | tf_op jit(solution)/shard_map/all_gather | solution.py:175
  7.9 115.7 %all-gather.14.cloned.1.call-start = ((), (), s32[]{:S(2)}) async-start(), calls=%async_computation.16 | async-start | bytes 1216512 | tf_op jit(solution)/shard_map/all_gather | solution.py:176
  8.7 170.9 %all-gather.10.cloned.1.call-start = ((), (), s32[]{:S(2)}) async-start(), calls=%async_computation.14 | async-start | bytes 1216512 | tf_op jit(solution)/shard_map/all_gather | solution.py:177
  9.4 318.8 %all-gather.16.cloned.1.call-start = ((), (), s32[]{:S(2)}) async-start(), calls=%async_computation.17 | async-start | bytes 1671168 | tf_op jit(solution)/shard_map/all_gather | solution.py:21
  11.5 2.7 copy-start.34
  74.9 48.8 %copy-start.14 = (bf16[1,512,768]{2,1,0:T(8,128)(2,1)S(1)}, bf16[1,512,768]{2,1,0:T(8,128)(2,1)}, u32[]{:S(2)}) copy-start(bf16[1,512,768]{2,1,0:T(8,128)(2,1)} %param.23) | copy-start | bytes 2359300
  186.4 8.6 copy-start
  195.5 6.3 copy-start.66
  195.5 47.5 %copy-start.58 = (bf16[24]{0:T(256)(128)(2,1)S(1)}, bf16[24]{0:T(256)(128)(2,1)}, u32[]{:S(2)}) copy-start(bf16[24]{0:T(256)(128)(2,1)} %param.33) | copy-start | bytes 148
  195.5 47.7 %copy-start.59 = (bf16[24]{0:T(256)(128)(2,1)S(1)}, bf16[24]{0:T(256)(128)(2,1)}, u32[]{:S(2)}) copy-start(bf16[24]{0:T(256)(128)(2,1)} %param.34) | copy-start | bytes 148
  195.6 47.9 %copy-start.60 = (bf16[24]{0:T(256)(128)(2,1)S(1)}, bf16[24]{0:T(256)(128)(2,1)}, u32[]{:S(2)}) copy-start(bf16[24]{0:T(256)(128)(2,1)} %param.32) | copy-start | bytes 148
  195.6 48.2 %copy-start.61 = (bf16[24]{0:T(256)(128)(2,1)S(1)}, bf16[24]{0:T(256)(128)(2,1)}, u32[]{:S(2)}) copy-start(bf16[24]{0:T(256)(128)(2,1)} %param.35) | copy-start | bytes 148
  195.6 48.4 %copy-start.62 = (bf16[24]{0:T(256)(128)(2,1)S(1)}, bf16[24]{0:T(256)(128)(2,1)}, u32[]{:S(2)}) copy-start(bf16[24]{0:T(256)(128)(2,1)} %param.36) | copy-start | bytes 148
  195.6 48.6 %copy-start.63 = (bf16[96]{0:T(256)(128)(2,1)S(1)}, bf16[96]{0:T(256)(128)(2,1)}, u32[]{:S(2)}) copy-start(bf16[96]{0:T(256)(128)(2,1)} %param.30) | copy-start | bytes 580
  197.6 148.8 %all-gather.18.cloned.1.call-start = ((), (), s32[]{:S(2)}) async-start(), calls=%async_computation.18 | async-start | bytes 1216512 | tf_op jit(solution)/shard_map/all_gather | solution.py:178
  198.2 178.0 %all-gather.20.cloned.1.call-start = ((), (), s32[]{:S(2)}) async-start(), calls=%async_computation.19 | async-start | bytes 4866048 | tf_op jit(solution)/shard_map/all_gather | solution.py:179
  198.8 242.8 %all-gather.22.cloned.1.call-start = ((), (), s32[]{:S(2)}) async-start(), calls=%async_computation.20 | async-start | bytes 4866048 | tf_op jit(solution)/shard_map/all_gather | solution.py:181
  342.0 6.4 all-to-all-start.3
  346.3 218.7 %all-gather.24.cloned.1.call-start = ((), (), s32[]{:S(2)}) async-start(), calls=%async_computation.21 | async-start | bytes 1671168 | tf_op jit(solution)/shard_map/all_gather | solution.py:21
  351.0 25.2 %copy-start.42 = (f32[768]{0:T(1024)S(1)}, f32[768]{0:T(1024)}, u32[]{:S(2)}) copy-start(f32[768]{0:T(1024)} %convert_element_type.312) | copy-start | bytes 9220
  351.0 25.2 %copy-start.51 = (f32[768]{0:T(1024)S(1)}, f32[768]{0:T(1024)}, u32[]{:S(2)}) copy-start(f32[768]{0:T(1024)} %convert_element_type.313) | copy-start | bytes 9220
  351.1 114.9 %copy-start.36 = (f32[512]{0:T(512)}, f32[512]{0:T(512)S(1)}, u32[]{:S(2)}) copy-start(f32[512]{0:T(512)S(1)} %broadcast_multiply_fusion.5) | copy-start | bytes 6148
  352.5 113.5 %copy-start.49 = (f32[512]{0:T(512)}, f32[512]{0:T(512)S(1)}, u32[]{:S(2)}) copy-start(f32[512]{0:T(512)S(1)} %add_rsqrt_fusion.1) | copy-start | bytes 6148
  352.5 89.1 %copy-start.46 = (f32[3072]{0:T(1024)S(1)}, f32[3072]{0:T(1024)}, u32[]{:S(2)}) copy-start(f32[3072]{0:T(1024)} %convert_element_type.315) | copy-start | bytes 36868
  352.5 89.1 %copy-start.53 = (f32[768]{0:T(1024)S(1)}, f32[768]{0:T(1024)}, u32[]{:S(2)}) copy-start(f32[768]{0:T(1024)} %convert_element_type.317) | copy-start | bytes 9220
  441.6 13.5 %copy-start.67 = (f32[512,3072]{1,0:T(8,128)S(1)}, f32[512,3072]{1,0:T(8,128)}, u32[]{:S(2)}) copy-start(f32[512,3072]{1,0:T(8,128)} %fusion.144) | copy-start | bytes 18874372
  451.7 3.5 copy-start.55
  453.0 9.3 slice-start
  455.1 7.2 copy-start.25
  455.1 7.1 copy-start.17
  455.1 7.2 slice-start.1
  462.3 3.7 copy-start.68
  468.5 7.8 copy-start.29
  486.6 3.4 copy-start.38
  502.0 3.4 copy-start.38
  508.2 255.9 %reduce-scatter.13.cloned.1.call-start = ((), (), s32[]{:S(2)}) async-start(), calls=%async_computation.22 | async-start | bytes 2433024 | tf_op jit(solution)/shard_map/reduce_scatter | solution.py:399
  552.4 12.7 copy-start.65
  552.4 221.0 %reduce-scatter.23.cloned.1.call-start = ((), (), s32[]{:S(2)}) async-start(), calls=%async_computation.27 | async-start | bytes 2433024
  565.1 39.3 %copy-start.33 = (f32[2,512]{1,0:T(2,128)S(1)}, f32[2,512]{1,0:T(2,128)}, u32[]{:S(2)}) copy-start(f32[2,512]{1,0:T(2,128)} %get-tuple-element.670) | copy-start | bytes 12292
  607.6 4.5 copy-start.15
  617.5 259.9 %reduce-scatter.19.cloned.1.call-start = ((), (), s32[]{:S(2)}) async-start(), calls=%async_computation.25 | async-start | bytes 2433024
  621.5 3.5 copy-start.11
  640.9 3.3 copy-start.40
  640.9 4.0 copy-start.3
  684.9 297.1 %reduce-scatter.21.cloned.1.call-start = ((), (), s32[]{:S(2)}) async-start(), calls=%async_computation.26 | async-start | bytes 2433024
  695.3 428.0 %reduce-scatter.15.cloned.1.call-start = ((), (), s32[]{:S(2)}) async-start(), calls=%async_computation.23 | async-start | bytes 9732096 | tf_op jit(solution)/shard_map/reduce_scatter | solution.py:400
  704.0 561.3 %reduce-scatter.17.cloned.1.call-start = ((), (), s32[]{:S(2)}) async-start(), calls=%async_computation.24 | async-start | bytes 9732096 | tf_op jit(solution)/shard_map/reduce_scatter | solution.py:402
  715.6 42.4 %copy-start.22 = (bf16[2,512,384]{1,2,0:T(8,128)(2,1)S(1)}, bf16[2,512,384]{1,2,0:T(8,128)(2,1)}, u32[]{:S(2)}) copy-start(bf16[2,512,384]{1,2,0:T(8,128)(2,1)} %copy-done.21) | copy-start | bytes 2359300
  (51 other events, 73.8 us)
Sparse Core Ops, SparseCore 0:
  10.9 56.7 all-gather.11
  70.6 52.9 all-gather.13
  126.5 52.9 all-gather.9
  197.7 57.4 all-gather.15
  258.0 52.9 all-gather.17
  313.7 62.4 all-gather.19
  379.1 62.4 all-gather.21
  508.3 56.6 all-gather.23
  570.9 97.8 reduce-scatter.12
  675.4 97.9 reduce-scatter.22
  779.3 98.1 reduce-scatter.18
  884.0 97.9 reduce-scatter.20
  988.5 134.6 reduce-scatter.14
  1130.6 134.6 reduce-scatter.16
where the time goes:
time: 1280 us; the launch traced here: 1270 us
  waiting for transfers between devices  747 us (58%)
  blocking collectives  227 us (18%)
  local copies, waits for them, and re-layouts  115 us (9%)
  matrix products  110 us (9%)
  other arithmetic  40 us (3%)
  between operations  16.8 us (1%)
    unnamed x17, waiting for transfers between devices  222 us
    reduce_scatter x1, waiting for transfers between devices, local(): lax.psum_scatter(grad_down, ('head', 'blk'), scatter_dimension=0, tiled=T...  142 us
    reduce_scatter x1, waiting for transfers between devices, local(): lax.psum_scatter(grad_up, ('head', 'blk'), scatter_dimension=0, tiled=True)  141 us
    unnamed x3, blocking collectives  115 us
    all_gather x2, blocking collectives, prefix(): lax.all_gather(a.astype(kind), axis)  78.2 us
    all_gather x1, waiting for transfers between devices, local(): lax.all_gather(w_down, ('head', 'blk'), axis=0, tiled=True)  57.2 us
    all_gather x1, waiting for transfers between devices, local(): lax.all_gather(w_query, ('head', 'blk'), axis=0, tiled=True)  53.5 us
    all_gather x1, waiting for transfers between devices, local(): lax.all_gather(w_value, ('head', 'blk'), axis=0, tiled=True)  46.7 us
  transfers between devices with their start and end apart: 15, of which 12 were waited for; matrix products, arithmetic and copies ran while one was open for 14% of the time, Pallas kernels for 0%

commit v1 on v0

v1 whole, which is shorter than its diff:
```python
import functools

import jax
import jax.numpy as jnp
from jax import lax
from jax.experimental import pallas as pl
from jax.experimental.pallas import tpu as pltpu
from jax.sharding import PartitionSpec as P

HEADS = 12
HEAD_DIM = 64
SUB = 512
PAIRS = HEADS // 2

eps = 1e-05
half_pi = 1.5707963267948966
f32 = jnp.float32
bf16 = jnp.bfloat16
MESH = pl.DeviceIdType.MESH
VMEM_BYTES = 58 << 20


class Grid:
    def __init__(self, chips):
        if chips == 16:
            self.inner, self.a, self.n, self.strides = 1, 4, 2, (1, 2)
            self.line = ((2, 1), (2, 2), (4, 4))
        elif chips == 128:
            self.inner, self.a, self.n, self.strides = 8, 1, 4, (1, 4)
            self.line = ((8, 1), (4, 8), (4, 32))
        else:
            raise ValueError(chips)
        self.groups = 16

    def lanes(self):
        return [
            [group * self.inner + lane for lane in range(self.inner)]
            for group in range(self.groups)
        ]


class Place:
    def __init__(self, grid):
        self.grid = grid
        self.core = lax.axis_index("head")
        self.blk = lax.axis_index("blk")
        group = self.blk // grid.inner
        self.lane = self.blk - group * grid.inner
        n, (near, far) = grid.n, grid.strides
        first = group // near % n
        second = group // far % n
        self.a = group // (n * n)
        flip = self.core == 0
        self.b = jnp.where(flip, first, second)
        self.c = jnp.where(flip, second, first)
        self.step_b = jnp.where(flip, near, far)
        self.step_c = jnp.where(flip, far, near)
        self.me = group

    def shard(self, a, b, c):
        return a * (self.grid.n * self.grid.n) + b * self.step_b + c * self.step_c

    def device(self, shard):
        return (self.core, shard * self.grid.inner + self.lane)

    def turn_a(self, d):
        return (self.a + d) % self.grid.a

    def turn_b(self, d):
        return (self.b + d) % self.grid.n

    def turn_c(self, d):
        return (self.c + d) % self.grid.n

    def peers_a(self):
        return [
            self.device(self.shard(self.turn_a(d), self.b, self.c))
            for d in range(1, self.grid.a)
        ]

    def peers_b(self):
        return [
            self.device(self.shard(self.a, self.turn_b(d), self.c))
            for d in range(1, self.grid.n)
        ]

    def peers_c(self):
        return [
            self.device(self.shard(self.a, self.b, self.turn_c(d)))
            for d in range(1, self.grid.n)
        ]

    def partner(self):
        return (1 - self.core, self.blk)


def greet(peers):
    barrier = pltpu.get_barrier_semaphore()
    for peer in peers:
        pl.semaphore_signal(barrier, inc=1, device_id=peer, device_id_type=MESH)
    pl.semaphore_wait(barrier, len(peers))


def send(src, dst, sent, got, device):
    pltpu.make_async_remote_copy(
        src_ref=src,
        dst_ref=dst,
        send_sem=sent,
        recv_sem=got,
        device_id=device,
        device_id_type=MESH,
    ).start()


def await_bytes(ref, sem):
    pltpu.make_async_copy(ref, ref, sem).wait()


def params(number=None):
    if number is None:
        return pltpu.CompilerParams(vmem_limit_bytes=VMEM_BYTES)
    return pltpu.CompilerParams(
        collective_id=number, has_side_effects=True, vmem_limit_bytes=VMEM_BYTES
    )


HBM_SPEC = pl.BlockSpec(memory_space=pltpu.HBM)
VMEM_SPEC = pl.BlockSpec(memory_space=pltpu.VMEM)


def vector_sum(place, vec, total, slots, sent, got):
    total[...] = vec[...]
    steps = (
        [place.partner()],
        place.peers_b(),
        place.peers_c(),
        place.peers_a(),
    )
    base = 0
    for number, peers in enumerate(steps):
        if not peers:
            continue
        for d, peer in enumerate(peers):
            send(total, slots.at[base + d], sent.at[number], got.at[number], peer)
        view = slots.at[pl.ds(base, len(peers))]
        await_bytes(view, got.at[number])
        await_bytes(view, sent.at[number])
        value = total[...]
        for d in range(len(peers)):
            value = value + slots[base + d]
        total[...] = value
        base += len(peers)


def gather_kernel(grid, units, count, *refs):
    shards, vec = refs[:count], refs[count]
    full, total = refs[count + 1 : 2 * count + 1], refs[2 * count + 1]
    slots, own, out_sem, got_a, got_b, got_bz, got_c, pair_out, got_p, vs, vg = refs[2 * count + 2 :]
    place = Place(grid)
    na, n = grid.a, grid.n
    greet(place.peers_a() + place.peers_b() + place.peers_c() + [place.partner()])
    core, partner = place.core, place.partner()

    def piece(u):
        w, r0, r, c0, c = units[u]
        return shards[w].at[pl.ds(r0, r), pl.ds(c0, c)]

    def slot(u, s):
        w, r0, r, c0, c = units[u]
        return full[w].at[core, s, pl.ds(r0, r), pl.ds(c0, c)]

    def many(u, k):
        w, r0, r, c0, c = units[u]
        return full[w].at[core, pl.ds(0, k), pl.ds(r0, r), pl.ds(c0, c)]

    def pass_on(u, s, peers, got):
        for peer in peers:
            send(slot(u, s), slot(u, s), out_sem.at[u], got.at[u], peer)

    def start(u):
        pltpu.make_async_copy(piece(u), slot(u, place.me), own.at[u]).start()
        for peers, got in (
            (place.peers_a(), got_a),
            (place.peers_b(), got_b),
            (place.peers_c(), got_c),
        ):
            for peer in peers:
                send(piece(u), slot(u, place.me), out_sem.at[u], got.at[u], peer)
        send(piece(u), slot(u, place.me), pair_out.at[u], got_p.at[u], partner)

    def after_a(u):
        if na > 1:
            await_bytes(many(u, na - 1), got_a.at[u])
        for d in range(1, na):
            pass_on(u, place.shard(place.turn_a(d), place.b, place.c), place.peers_b(), got_bz)
        await_bytes(many(u, n - 1), got_b.at[u])
        for d in range(1, n):
            pass_on(u, place.shard(place.a, place.turn_b(d), place.c), place.peers_c(), got_c)
        for d in range(1, na):
            pass_on(u, place.shard(place.turn_a(d), place.b, place.c), place.peers_c(), got_c)

    def after_b(u):
        if na > 1:
            await_bytes(many(u, (na - 1) * (n - 1)), got_bz.at[u])
        for d in range(na):
            for e in range(n):
                s = place.shard(place.turn_a(d), place.turn_b(e), place.c)
                if d > 0 and e > 0:
                    pass_on(u, s, place.peers_c(), got_c)
                if d > 0 or e > 0:
                    send(slot(u, s), slot(u, s), pair_out.at[u], got_p.at[u], partner)

    def after_c(u):
        await_bytes(many(u, na * n * (n - 1)), got_c.at[u])
        for d in range(na):
            for e in range(n):
                for f in range(1, n):
                    s = place.shard(place.turn_a(d), place.turn_b(e), place.turn_c(f))
                    send(slot(u, s), slot(u, s), pair_out.at[u], got_p.at[u], partner)

    ahead = 4
    size = len(units)
    for u in range(min(ahead, size)):
        start(u)
    for step in range(size + 2):
        if step < size:
            after_a(step)
        if step + ahead < size:
            start(step + ahead)
        if 0 <= step - 1 < size:
            after_b(step - 1)
        if 0 <= step - 2 < size:
            after_c(step - 2)
    vector_sum(place, vec, total, slots, vs, vg)
    sends = (na - 1) + 2 * (n - 1) + (na - 1) * (n - 1) + (n - 1) * (na * n - 1)
    for u in range(size):
        await_bytes(many(u, 1), own.at[u])
        await_bytes(many(u, 16), got_p.at[u])
        await_bytes(many(u, 16), pair_out.at[u])
        left = sends
        while left > 0:
            await_bytes(many(u, min(left, 16)), out_sem.at[u])
            left -= 16


def split_units(shapes):
    units = []
    for w, (r, c) in enumerate(shapes):
        if c > 1024:
            for part in range(2):
                units.append((w, 0, r, part * c // 2, c // 2))
        elif r > 48:
            for part in range(2):
                units.append((w, part * r // 2, r // 2, 0, c))
        else:
            units.append((w, 0, r, 0, c))
    return tuple(units)


def gather_weights(grid, weights, vec):
    shapes = [w.shape for w in weights]
    units = split_units(shapes)
    size = len(units)
    dma = pltpu.SemaphoreType.DMA((size,))
    peers = 1 + 2 * (grid.n - 1) + (grid.a - 1)
    out = pl.pallas_call(
        functools.partial(gather_kernel, grid, units, len(weights)),
        out_shape=tuple(jax.ShapeDtypeStruct((2, 16) + s, bf16) for s in shapes)
        + (jax.ShapeDtypeStruct(vec.shape, f32),),
        in_specs=[HBM_SPEC] * len(weights) + [VMEM_SPEC],
        out_specs=(HBM_SPEC,) * len(weights) + (VMEM_SPEC,),
        scratch_shapes=[pltpu.VMEM((peers,) + vec.shape, f32)]
        + [dma] * 8
        + [pltpu.SemaphoreType.DMA((4,))] * 2,
        compiler_params=params(1),
        name="gather_weights",
    )(*weights, vec)
    return [o.reshape(32 * s[0], s[1]) for o, s in zip(out, shapes)], out[-1]


def scatter_kernel(grid, units, count, *refs):
    grads, vec = refs[:count], refs[count]
    out, total = refs[count + 1 : 2 * count + 1], refs[2 * count + 1]
    rest = refs[2 * count + 2 :]
    size = len(units)
    acc, in_p, in_c, in_b, in_a, res = (rest[k * size : (k + 1) * size] for k in range(6))
    (slots, own, out_p, got_p, out_c, got_c, out_b, got_b, out_a, got_a, done, vs, vg) = rest[
        6 * size :
    ]
    place = Place(grid)
    na, n = grid.a, grid.n
    core = place.core
    greet(place.peers_a() + place.peers_b() + place.peers_c() + [place.partner()])

    def grad(u, side):
        w, r0, r, c0, c = units[u]
        return grads[w].at[side, :, pl.ds(r0, r), pl.ds(c0, c)]

    def add(u, s, value):
        acc[u][s] = (acc[u][s].astype(f32) + value.astype(f32)).astype(bf16)

    def start(u):
        send(grad(u, 1 - core), in_p[u], out_p.at[u], got_p.at[u], place.partner())
        pltpu.make_async_copy(grad(u, core), acc[u], own.at[u]).start()

    def after_p(u):
        await_bytes(in_p[u], got_p.at[u])
        await_bytes(acc[u], own.at[u])
        for f in list(range(1, n)) + [0]:

            def step(i, carry):
                s = place.shard(i // n, i % n, place.turn_c(f))
                add(u, s, in_p[u][s])
                if f > 0:
                    send(
                        acc[u].at[s],
                        in_c[u].at[f - 1, i],
                        out_c.at[u],
                        got_c.at[u],
                        place.peers_c()[f - 1],
                    )
                return carry

            lax.fori_loop(0, na * n, step, 0)

    def after_c(u):
        await_bytes(in_c[u], got_c.at[u])
        for e in list(range(1, n)) + [0]:

            def step(i, carry):
                s = place.shard(i, place.turn_b(e), place.c)
                j = i * n + place.turn_b(e)
                value = in_c[u][0, j].astype(f32)
                for f in range(1, n - 1):
                    value = value + in_c[u][f, j].astype(f32)
                add(u, s, value)
                if e > 0:
                    send(
                        acc[u].at[s],
                        in_b[u].at[e - 1, i],
                        out_b.at[u],
                        got_b.at[u],
                        place.peers_b()[e - 1],
                    )
                return carry

            lax.fori_loop(0, na, step, 0)

    def after_b(u):
        await_bytes(in_b[u], got_b.at[u])
        for d in list(range(1, na)) + [0]:
            i = place.turn_a(d)
            s = place.shard(i, place.b, place.c)
            value = in_b[u][0, i].astype(f32)
            for e in range(1, n - 1):
                value = value + in_b[u][e, i].astype(f32)
            add(u, s, value)
            if d > 0:
                send(acc[u].at[s], in_a[u].at[d - 1], out_a.at[u], got_a.at[u], place.device(s))

    def after_a(u):
        w, r0, r, c0, c = units[u]
        value = acc[u][place.me].astype(f32)
        if na > 1:
            await_bytes(in_a[u], got_a.at[u])
            for d in range(na - 1):
                value = value + in_a[u][d].astype(f32)
        res[u][...] = value
        pltpu.make_async_copy(res[u], out[w].at[pl.ds(r0, r), pl.ds(c0, c)], done.at[u]).start()

    for u in range(size):
        start(u)
    for step in range(size + 3):
        if step < size:
            after_p(step)
        if 0 <= step - 1 < size:
            after_c(step - 1)
        if 0 <= step - 2 < size:
            after_b(step - 2)
        if 0 <= step - 3 < size:
            after_a(step - 3)
    vector_sum(place, vec, total, slots, vs, vg)
    for u in range(size):
        await_bytes(in_p[u], out_p.at[u])
        await_bytes(in_c[u], out_c.at[u])
        await_bytes(in_b[u], out_b.at[u])
        if na > 1:
            await_bytes(in_a[u], out_a.at[u])
        await_bytes(res[u], done.at[u])


def scatter_grads(grid, grads, vec, shapes):
    units = split_units(shapes)
    size = len(units)
    na, n = grid.a, grid.n
    dma = pltpu.SemaphoreType.DMA((size,))

    def room(*lead):
        return [pltpu.VMEM(lead + (u[2], u[4]), bf16) for u in units]

    peers = 1 + 2 * (n - 1) + (na - 1)
    out = pl.pallas_call(
        functools.partial(scatter_kernel, grid, units, len(grads)),
        out_shape=tuple(jax.ShapeDtypeStruct(s, f32) for s in shapes)
        + (jax.ShapeDtypeStruct(vec.shape, f32),),
        in_specs=[HBM_SPEC] * len(grads) + [VMEM_SPEC],
        out_specs=(HBM_SPEC,) * len(grads) + (VMEM_SPEC,),
        scratch_shapes=room(16)
        + room(16)
        + room(n - 1, na * n)
        + room(n - 1, na)
        + room(max(na - 1, 1))
        + [pltpu.VMEM((u[2], u[4]), f32) for u in units]
        + [pltpu.VMEM((peers,) + vec.shape, f32)]
        + [dma] * 10
        + [pltpu.SemaphoreType.DMA((4,))] * 2,
        compiler_params=params(2),
        name="scatter_grads",
    )(*[g.reshape((2, 16) + s) for g, s in zip(grads, shapes)], vec)
    return out[:-1], out[-1]


def fold(state, total, state_next, total_next):
    keep = total_next[2:3, :]
    row = lax.broadcasted_iota(jnp.int32, total_next.shape, 0)
    return (
        keep[:, :128] * state + state_next,
        keep * total + jnp.where(row == 2, 0.0, total_next),
    )


def neutral(state_shape, total_shape):
    row = lax.broadcasted_iota(jnp.int32, total_shape, 0)
    return jnp.zeros(state_shape, f32), jnp.where(row == 2, 1.0, 0.0).astype(f32)


def state_kernel(grid, backward, *refs):
    state, total, entering, entering_total = refs[:4]
    own_s, pair_s, pair_t, fin_s, fin_t = refs[4:9]
    lines = len(grid.line)
    slot_s, slot_t, exc_s, exc_t = (refs[9 + k * lines : 9 + (k + 1) * lines] for k in range(4))
    so, sg, to, tg = refs[9 + 4 * lines :]
    core, blk = lax.axis_index("head"), lax.axis_index("blk")
    partner = (1 - core, blk)
    places = [blk // stride % size for size, stride in grid.line]

    def line_peers(d):
        size, stride = grid.line[d]
        at = places[d]
        return [(core, blk + ((at + k) % size - at) * stride) for k in range(1, size)]

    greet([partner] + [p for d in range(lines) for p in line_peers(d)])
    half = pl.ds(core * 3, 3)
    wide = pl.ds(pl.multiple_of(core * 384, 384), 384)
    own_s[...] = state[...].astype(bf16)
    send(own_s, pair_s, so.at[0], sg.at[0], partner)
    send(total, pair_t, to.at[0], tg.at[0], partner)
    await_bytes(pair_s, sg.at[0])
    await_bytes(pair_t, tg.at[0])
    first = (core == 1) if backward else (core == 0)
    mine = state[half], total[:, wide]
    theirs = pair_s[half].astype(f32), pair_t[:, wide]
    ahead = [jnp.where(first, m, t) for m, t in zip(mine, theirs)]
    behind = [jnp.where(first, t, m) for m, t in zip(mine, theirs)]
    run_s, run_t = fold(*ahead, *behind)
    for d in range(lines):
        size, stride = grid.line[d]
        at = places[d]
        slot_s[d][at] = run_s.astype(bf16)
        slot_t[d][at] = run_t
        for peer in line_peers(d):
            send(slot_s[d].at[at], slot_s[d].at[at], so.at[d + 1], sg.at[d + 1], peer)
            send(slot_t[d].at[at], slot_t[d].at[at], to.at[d + 1], tg.at[d + 1], peer)
        await_bytes(slot_s[d].at[pl.ds(0, size - 1)], sg.at[d + 1])
        await_bytes(slot_t[d].at[pl.ds(0, size - 1)], tg.at[d + 1])
        run_s, run_t = neutral(run_s.shape, run_t.shape)
        part_s, part_t = run_s, run_t
        for j in range(size - 1, -1, -1) if backward else range(size):
            next_s, next_t = slot_s[d][j].astype(f32), slot_t[d][j]
            before = (j > at) if backward else (j < at)
            added_s, added_t = fold(part_s, part_t, next_s, next_t)
            part_s = jnp.where(before, added_s, part_s)
            part_t = jnp.where(before, added_t, part_t)
            if d < lines - 1:
                run_s, run_t = fold(run_s, run_t, next_s, next_t)
        exc_s[d][...] = part_s
        exc_t[d][...] = part_t
    part_s, part_t = exc_s[lines - 1][...], exc_t[lines - 1][...]
    for d in range(lines - 2, -1, -1):
        part_s, part_t = fold(part_s, part_t, exc_s[d][...], exc_t[d][...])
    fin_s[half] = part_s.astype(bf16)
    fin_t[core] = part_t
    send(fin_s.at[half], fin_s.at[half], so.at[lines + 1], sg.at[lines + 1], partner)
    send(fin_t.at[core], fin_t.at[core], to.at[lines + 1], tg.at[lines + 1], partner)
    await_bytes(fin_s.at[half], sg.at[lines + 1])
    await_bytes(fin_t.at[core], tg.at[lines + 1])
    chip_s = fin_s[...].astype(f32)
    chip_t = jnp.concatenate([fin_t[0], fin_t[1]], axis=1)
    after_s, after_t = fold(chip_s, chip_t, pair_s[...].astype(f32), pair_t[...])
    entering[...] = jnp.where(first, chip_s, after_s).astype(bf16)
    entering_total[...] = jnp.where(first, chip_t, after_t)
    await_bytes(pair_s, so.at[0])
    await_bytes(pair_t, to.at[0])
    for d in range(lines):
        size, stride = grid.line[d]
        await_bytes(slot_s[d].at[pl.ds(0, size - 1)], so.at[d + 1])
        await_bytes(slot_t[d].at[pl.ds(0, size - 1)], to.at[d + 1])
    await_bytes(fin_s.at[half], so.at[lines + 1])
    await_bytes(fin_t.at[core], to.at[lines + 1])


def exchange_states(grid, state, total, backward):
    lines = grid.line
    sem = pltpu.SemaphoreType.DMA((len(lines) + 2,))
    return pl.pallas_call(
        functools.partial(state_kernel, grid, backward),
        out_shape=(
            jax.ShapeDtypeStruct((PAIRS, 128, 128), bf16),
            jax.ShapeDtypeStruct((8, 768), f32),
        ),
        in_specs=[VMEM_SPEC] * 2,
        out_specs=(VMEM_SPEC,) * 2,
        scratch_shapes=[
            pltpu.VMEM((PAIRS, 128, 128), bf16),
            pltpu.VMEM((PAIRS, 128, 128), bf16),
            pltpu.VMEM((8, 768), f32),
            pltpu.VMEM((PAIRS, 128, 128), bf16),
            pltpu.VMEM((2, 8, 384), f32),
        ]
        + [pltpu.VMEM((size, 3, 128, 128), bf16) for size, _ in lines]
        + [pltpu.VMEM((size, 8, 384), f32) for size, _ in lines]
        + [pltpu.VMEM((3, 128, 128), f32) for _ in lines]
        + [pltpu.VMEM((8, 384), f32) for _ in lines]
        + [sem] * 4,
        compiler_params=params(4 if backward else 3),
        name="exchange_states",
    )(state, total)


def dot(a, b, contract=((1,), (0,))):
    return lax.dot_general(a, b, (contract, ((), ())), preferred_element_type=f32)


def tall(row):
    return jnp.transpose(jnp.broadcast_to(row, (128, row.shape[1])))


def lane_side(shape):
    return lax.broadcasted_iota(jnp.int32, shape, 1) < HEAD_DIM


def ones_by_head():
    rows = lax.broadcasted_iota(jnp.int32, (128, 128), 0) < HEAD_DIM
    return jnp.where(rows == lane_side((128, 128)), 1.0, 0.0).astype(bf16)


def widen(compact):
    side = lane_side((64, 128))
    zero = jnp.zeros((64, 128), compact.dtype)
    parts = []
    for k in range(2):
        piece = compact[64 * k : 64 * k + 64]
        parts += [jnp.where(side, piece, zero), jnp.where(side, zero, piece)]
    return jnp.concatenate(parts, axis=0)


def compact_of(full):
    return jnp.where(lane_side((64, 128)), full[:64], full[64:])


def sum_by_head(value):
    high = value.astype(bf16)
    low = (value - high.astype(f32)).astype(bf16)
    ones = ones_by_head()
    return dot(jnp.concatenate([high, low], axis=1), jnp.concatenate([ones, ones], axis=0))


def position_terms(row, reach):
    place = row.astype(f32)
    angle = place * (half_pi / reach)
    cosine, sine = tall(jnp.cos(angle)), tall(jnp.sin(angle))
    column = tall(place)
    index = lax.broadcasted_iota(jnp.int32, column.shape, 0).astype(f32)
    use = (column > index).astype(f32)
    last = column[SUB - 1 : SUB, :]
    tail = ((SUB - 1) - index <= last).astype(f32)
    keep = (last >= SUB).astype(f32)
    return cosine, sine, use, tail, keep


def projections_kernel(reach, tok, wq, wk, wv, pos, q_out, k_out, v_out, sq_out, sk_out, state, total):
    rows = tok[...]
    cosine, sine, use, tail, keep = position_terms(pos[...], reach)
    for weight, raw, soft in ((wq, q_out, sq_out), (wk, k_out, sk_out), (wv, v_out, None)):
        for part in range(3):
            cols = slice(256 * part, 256 * part + 256)
            value = dot(rows, weight[:, cols]).astype(bf16)
            raw[:, cols] = value
            if soft is not None:
                wide = value.astype(f32)
                soft[:, cols] = jnp.maximum(wide, 0.0) + jnp.log1p(jnp.exp(-jnp.abs(wide)))
    for p in range(PAIRS):
        cols = slice(128 * p, 128 * p + 128)
        soft = sk_out[:, cols] * tail
        value = v_out[:, cols]
        for k, wave in enumerate((cosine, sine)):
            feature = (soft * wave).astype(bf16)
            state[p, 64 * k : 64 * k + 64, :] = compact_of(dot(feature, value, ((0,), (0,))))
            total[k : k + 1, cols] = jnp.sum(feature.astype(f32), axis=0, keepdims=True)
        total[2:3, cols] = keep
        total[3:8, cols] = jnp.zeros((5, 128), f32)


def mask_of(row, reach, flipped):
    place = row.astype(f32)
    angle = place * (half_pi / reach)
    cos_row, sin_row = jnp.cos(angle), jnp.sin(angle)
    across = lambda r: jnp.broadcast_to(r, (SUB, SUB))
    down = lambda r: jnp.transpose(across(r))
    i = lax.broadcasted_iota(jnp.int32, (SUB, SUB), 1 if flipped else 0)
    j = lax.broadcasted_iota(jnp.int32, (SUB, SUB), 0 if flipped else 1)
    spot = across(place) if flipped else down(place)
    seen = (j <= i) & ((i - j).astype(f32) <= spot)
    wave = down(cos_row) * across(cos_row) + down(sin_row) * across(sin_row)
    return jnp.where(seen, wave, 0.0)


def attend_kernel(reach, pos, sq, sk, v, entering, entering_total, mixed, inverse, mask):
    mask[...] = mask_of(pos[...], reach, False)
    cosine, sine, use, tail, keep = position_terms(pos[...], reach)
    ones = jnp.ones((SUB, 128), bf16)
    side = lane_side((SUB, 128))

    def one(p, carry):
        cols = pl.ds(pl.multiple_of(128 * p, 128), 128)
        soft = sq[:, cols]
        key = sk[:, cols].astype(bf16)
        values = jnp.concatenate([v[:, cols], ones], axis=1)
        qc, qs = soft * (cosine * use), soft * (sine * use)
        wide = widen(entering[p])
        num = dot(jnp.concatenate([qc, qs], axis=1).astype(bf16), wide)
        den = sum_by_head(qc * entering_total[0:1, cols] + qs * entering_total[1:2, cols])
        query = soft.astype(bf16)
        zero = jnp.zeros_like(query)
        outs = []
        for pick in (jnp.where(side, query, zero), jnp.where(side, zero, query)):
            top = (dot(pick[:256], key[:256], ((1,), (1,))) * mask[:256, :256]).astype(bf16)
            low = (dot(pick[256:], key, ((1,), (1,))) * mask[256:, :]).astype(bf16)
            outs.append(jnp.concatenate([dot(top, values[:256]), dot(low, values)], axis=0))
        num = num + jnp.where(side, outs[0][:, :128], outs[1][:, :128])
        den = den + jnp.where(side, outs[0][:, 128:], outs[1][:, 128:])
        inv = 1.0 / den
        inverse[:, cols] = inv
        mixed[:, cols] = (num * inv).astype(bf16)
        return carry

    lax.fori_loop(0, PAIRS, one, 0)


def use_kernel(reach, pos, sq, mixed, inverse, grad_mixed, g_out, e_out, state, total):
    cosine, sine, use, tail, keep = position_terms(pos[...], reach)

    def one(p, carry):
        cols = pl.ds(pl.multiple_of(128 * p, 128), 128)
        grad = grad_mixed[:, cols].astype(f32)
        inv = inverse[:, cols]
        g = (grad * inv).astype(bf16)
        e = -(sum_by_head(grad * mixed[:, cols].astype(f32)) * inv)
        g_out[:, cols] = g
        e_out[:, cols] = e
        soft = sq[:, cols] * use
        for k, wave in enumerate((cosine, sine)):
            feature = (soft * wave).astype(bf16)
            state[p, 64 * k : 64 * k + 64, :] = compact_of(dot(feature, g, ((0,), (0,))))
            total[k : k + 1, cols] = jnp.sum(feature.astype(f32) * e, axis=0, keepdims=True)
        total[2:3, cols] = keep
        total[3:8, cols] = jnp.zeros((5, 128), f32)
        return carry

    lax.fori_loop(0, PAIRS, one, 0)


def back_kernel(
    reach, pos, q, k, v, sq, sk, g, e, entering, entering_total, later, later_total,
    grad_q, grad_k, grad_v, mask,
):
    mask[...] = mask_of(pos[...], reach, True)
    cosine, sine, use, tail, keep = position_terms(pos[...], reach)
    side = lane_side((SUB, 128))
    lane = lax.broadcasted_iota(jnp.int32, (SUB, 128), 1)

    def sigmoid(raw):
        return 1.0 / (1.0 + jnp.exp(-raw.astype(f32)))

    def one(p, carry):
        cols = pl.ds(pl.multiple_of(128 * p, 128), 128)
        soft_q, soft_k = sq[:, cols], sk[:, cols]
        query, key = soft_q.astype(bf16), soft_k.astype(bf16)
        value, gp, ep = v[:, cols], g[:, cols], e[:, cols]
        e_high = ep.astype(bf16)
        e_low = (ep - e_high.astype(f32)).astype(bf16)
        gx = jnp.concatenate([gp, jnp.where(lane % 2 == 0, e_high, e_low)], axis=1)
        zero = jnp.zeros_like(query)
        key_t = jnp.transpose(key)
        rows_q, parts_k, parts_v = [], [], []
        for h in range(2):
            mine = side if h == 0 else jnp.logical_not(side)
            pick = jnp.where(mine, key, zero)
            probe = jnp.where((lane == 64 * h) | (lane == 64 * h + 1), 1.0, 0.0).astype(bf16)
            vx = jnp.concatenate([jnp.where(mine, value, zero), probe], axis=1)
            w_top = (dot(pick[:256], query, ((1,), (1,))) * mask[:256, :]).astype(bf16)
            w_low = (dot(pick[256:], query[256:], ((1,), (1,))) * mask[256:, 256:]).astype(bf16)
            d_top = (dot(vx[:256], gx, ((1,), (1,))) * mask[:256, :]).astype(bf16)
            d_low = (dot(vx[256:], gx[256:], ((1,), (1,))) * mask[256:, 256:]).astype(bf16)
            parts_k.append(jnp.concatenate([dot(d_top, query), dot(d_low, query[256:])], axis=0))
            parts_v.append(jnp.concatenate([dot(w_top, gp), dot(w_low, gp[256:])], axis=0))
            slim = key_t[64 * h : 64 * h + 64]
            first = dot(slim[:, :256], d_top)
            second = dot(slim[:, 256:], d_low)
            rows_q.append(jnp.concatenate([first[:, :256], first[:, 256:] + second], axis=1))
        grad_soft_q = jnp.transpose(jnp.concatenate(rows_q, axis=0))
        grad_soft_k = jnp.where(side, parts_k[0], parts_k[1])
        grad_val = jnp.where(side, parts_v[0], parts_v[1])
        wide = widen(entering[p])
        through = dot(gp, wide, ((1,), (1,)))
        grad_soft_q = grad_soft_q + use * (
            cosine * (through[:, :128] + ep * entering_total[0:1, cols])
            + sine * (through[:, 128:] + ep * entering_total[1:2, cols])
        )
        wide = widen(later[p])
        through = dot(value, wide, ((1,), (1,)))
        grad_soft_k = grad_soft_k + tail * (
            cosine * (through[:, :128] + later_total[0:1, cols])
            + sine * (through[:, 128:] + later_total[1:2, cols])
        )
        soft = soft_k * tail
        feature = jnp.concatenate([soft * cosine, soft * sine], axis=1).astype(bf16)
        grad_val = grad_val + dot(feature, wide)
        grad_q[:, cols] = (grad_soft_q * sigmoid(q[:, cols])).astype(bf16)
        grad_k[:, cols] = (grad_soft_k * sigmoid(k[:, cols])).astype(bf16)
        grad_v[:, cols] = grad_val.astype(bf16)
        return carry

    lax.fori_loop(0, PAIRS, one, 0)


def call(kernel, outs, *args, scratch=(), name=None):
    return pl.pallas_call(
        kernel,
        out_shape=tuple(jax.ShapeDtypeStruct(s, d) for s, d in outs),
        in_specs=[VMEM_SPEC] * len(args),
        out_specs=(VMEM_SPEC,) * len(outs),
        scratch_shapes=list(scratch),
        compiler_params=params(),
        name=name,
    )(*args)


def norm_rows(values, gain_factor, shift_term):
    centered = values - jnp.mean(values, axis=-1, keepdims=True)
    inv_scale = lax.rsqrt(jnp.mean(centered * centered, axis=-1, keepdims=True) + eps)
    normed = centered * inv_scale
    return (normed * gain_factor + shift_term, normed, inv_scale)


def norm_back(grad_rows, normed, inv_scale, gain_factor):
    grad_norm = grad_rows * gain_factor
    inner_term = (
        grad_norm
        - jnp.mean(grad_norm, axis=-1, keepdims=True)
        - normed * jnp.mean(grad_norm * normed, axis=-1, keepdims=True)
    )
    return (inv_scale * inner_term, jnp.sum(grad_rows * normed, axis=0), jnp.sum(grad_rows, axis=0))


def local(
    inputs, positions, w_query, w_key, w_value, w_out, w_up, bias_up, w_down, bias_down,
    gain_mid, shift_mid, gain_out, shift_out, grad_out,
):
    chips = lax.axis_size("blk")
    grid = Grid(chips)
    devices = 2 * chips
    device = lax.axis_index("head") * chips + lax.axis_index("blk")
    tokens = inputs[0]
    width = tokens.shape[1]
    reach = float(SUB * devices)
    weights = [w_query, w_key, w_value, w_out, w_up, w_down]
    small = [bias_up, bias_down, gain_mid, shift_mid, gain_out, shift_out]

    def spread(piece):
        size = piece.shape[0]
        rows = lax.broadcasted_iota(jnp.int32, (size, size * devices), 0)
        cols = lax.broadcasted_iota(jnp.int32, (size, size * devices), 1)
        spot = (cols == rows + device * size).astype(bf16)
        return dot(piece[None], spot).reshape(-1, width)

    vec = jnp.concatenate([spread(piece) for piece in small] + [jnp.zeros((7, width), f32)])
    if grid.inner > 1:
        lanes = grid.lanes()
        weights = [
            lax.all_gather(w, "blk", axis=0, tiled=True, axis_index_groups=lanes) for w in weights
        ]
        vec = lax.psum(vec, "blk", axis_index_groups=lanes)
    shapes = [w.shape for w in weights]
    (wq, wk, wv, wo, wu, wd), vec = gather_weights(grid, weights, vec)
    lift_bias, drop_bias = vec[:4].reshape(-1), vec[4]
    mid_gain, mid_shift, end_gain, end_shift = vec[5], vec[6], vec[7], vec[8]

    square, wide = (SUB, width), (PAIRS, 128, 128)
    q, k, v, sq, sk, state, total = call(
        functools.partial(projections_kernel, reach),
        [(square, bf16)] * 3 + [(square, f32)] * 2 + [(wide, f32), ((8, width), f32)],
        tokens, wq, wk, wv, positions, name="projections",
    )
    entering, entering_total = exchange_states(grid, state, total, False)
    mixed, inverse = call(
        functools.partial(attend_kernel, reach),
        [(square, bf16), (square, f32)],
        positions, sq, sk, v, entering, entering_total,
        scratch=[pltpu.VMEM((SUB, SUB), f32)], name="attend",
    )
    middle = tokens.astype(f32) + dot(mixed, wo)
    mid_rows, normed_mid, scale_mid = norm_rows(middle, mid_gain, mid_shift)
    mid_rounded = mid_rows.astype(bf16)
    up_rows = dot(mid_rounded, wu) + lift_bias
    gelu_rows, gelu_back = jax.vjp(jax.nn.gelu, up_rows)
    active = gelu_rows.astype(bf16)
    after_ffn = mid_rows + dot(active, wd) + drop_bias
    result, normed_end, scale_end = norm_rows(after_ffn, end_gain, end_shift)
    output = result.astype(bf16)[None]
    grad_rows = grad_out[0].astype(f32)
    grad_after, grad_end_gain, grad_end_shift = norm_back(
        grad_rows, normed_end, scale_end, end_gain
    )
    grad_branch = grad_after.astype(bf16)
    grad_down = dot(active, grad_branch, ((0,), (0,))).astype(bf16)
    grad_drop = jnp.sum(grad_branch, axis=0, dtype=f32)
    grad_active = dot(grad_branch, wd, ((1,), (1,)))
    grad_lift_rows = gelu_back(grad_active)[0].astype(bf16)
    grad_up = dot(mid_rounded, grad_lift_rows, ((0,), (0,))).astype(bf16)
    grad_lift = jnp.sum(grad_lift_rows, axis=0, dtype=f32)
    grad_mid_rows = dot(grad_lift_rows, wu, ((1,), (1,))) + grad_after
    grad_middle, grad_mid_gain, grad_mid_shift = norm_back(
        grad_mid_rows, normed_mid, scale_mid, mid_gain
    )
    grad_attn = grad_middle.astype(bf16)
    grad_out_weight = dot(mixed, grad_attn, ((0,), (0,))).astype(bf16)
    grad_mixed = dot(grad_attn, wo, ((1,), (1,))).astype(bf16)
    g, e, state, total = call(
        functools.partial(use_kernel, reach),
        [(square, bf16), (square, f32), (wide, f32), ((8, width), f32)],
        positions, sq, mixed, inverse, grad_mixed, name="use",
    )
    later, later_total = exchange_states(grid, state, total, True)
    grad_q, grad_k, grad_v = call(
        functools.partial(back_kernel, reach),
        [(square, bf16)] * 3,
        positions, q, k, v, sq, sk, g, e, entering, entering_total, later, later_total,
        scratch=[pltpu.VMEM((SUB, SUB), f32)], name="back",
    )
    grad_weights = [dot(tokens, r, ((0,), (0,))).astype(bf16) for r in (grad_q, grad_k, grad_v)]
    grad_inputs = grad_middle
    for r, w in ((grad_q, wq), (grad_k, wk), (grad_v, wv)):
        grad_inputs = grad_inputs + dot(r, w, ((1,), (1,)))
    vec = jnp.concatenate(
        [
            grad_lift.reshape(-1, width),
            jnp.stack([grad_drop, grad_mid_gain, grad_mid_shift, grad_end_gain, grad_end_shift]),
            jnp.zeros((7, width), f32),
        ]
    )
    summed, vec = scatter_grads(
        grid, grad_weights + [grad_out_weight, grad_up, grad_down], vec, shapes
    )
    if grid.inner > 1:
        lanes = grid.lanes()
        summed = [
            lax.psum_scatter(
                s, "blk", scatter_dimension=0, tiled=True, axis_index_groups=lanes
            )
            for s in summed
        ]
        vec = lax.psum(vec, "blk", axis_index_groups=lanes)
    pieces = []
    flat = [vec[:4].reshape(-1)] + [vec[r] for r in range(4, 9)]
    for whole, piece in zip(flat, small):
        size = piece.shape[0]
        pieces.append(lax.dynamic_slice(whole, (device * size,), (size,)))
    g_q, g_k, g_v, g_o, g_u, g_d = summed
    return (
        output, grad_inputs[None], g_q, g_k, g_v, g_o, g_u, pieces[0], g_d, *pieces[1:],
    )


def solution(mesh):
    rows = P(("head", "blk"), None)
    ones = P(("head", "blk"))
    seq = P("blk", "head", None)
    in_specs = (
        seq, P("blk", "head"), rows, rows, rows, rows, rows, ones, rows, ones, ones, ones, ones,
        ones, seq,
    )
    out_specs = (
        seq, seq, rows, rows, rows, rows, rows, ones, rows, ones, ones, ones, ones, ones,
    )
    return jax.shard_map(local, mesh=mesh, in_specs=in_specs, out_specs=out_specs, check_vma=False)
```

time: 1280 us -> 345 us (0.27)
  waiting for transfers between devices: 747 us -> 0 us
  Pallas kernels: 0 us -> 260 us
  blocking collectives: 227 us -> 0 us
  local copies, waits for them, and re-layouts: 115 us -> 22.7 us
  matrix products: 110 us -> 57.4 us
  other arithmetic: 40 us -> 3.62 us
  between operations: 16.8 us -> 1.07 us
    reduce_scatter x3 -> x0, waiting for transfers between devices: 283 us -> none  [the longest x1 142 us: local(): lax.psum_scatter(grad_down, ('head', 'blk'), scatter_dimension=0, tiled=T...]
    pallas_call x0 -> x8, Pallas kernels: none -> 260 us  [the longest x1 89.8 us: scatter_grads(): pl.pallas_call(functools.partial(scatter_kernel, grid, units, len(grads))...]
    all_gather x8 -> x0, waiting for transfers between devices: 240 us -> none  [the longest x1 57.2 us: local(): lax.all_gather(w_down, ('head', 'blk'), axis=0, tiled=True)]
    unnamed x17 -> x0, waiting for transfers between devices: 222 us -> none
    unnamed x3 -> x0, blocking collectives: 115 us -> none
    all_gather x3 -> x0, blocking collectives: 80.3 us -> none  [the longest x2 78.2 us: prefix(): lax.all_gather(a.astype(kind), axis)]
    dot_general x51 -> x21, matrix products: 110 us -> 57.4 us  [dot(): lax.dot_general(a, b, (contract, ((), ())), preferred_element_type=f32)]
    all_to_all x7 -> x0, blocking collectives: 32 us -> none  [the longest x1 5.45 us: local(): lax.all_to_all(grad_mixed, 'head', split_axis=1, concat_axis=0, tiled=True)]
  transfers between devices with their start and end apart: 15 -> 0, of which waited for: 12 -> 0; matrix products, arithmetic and copies ran while one was open for 14% -> 0% of each run, Pallas kernels for 0% -> 0%
where the time goes in v1:
time: 345 us; the launch traced here: 344 us
  Pallas kernels  260 us (75%)
  matrix products  57.4 us (17%)
  local copies, waits for them, and re-layouts  22.7 us (7%)
  other arithmetic  3.62 us (1%)
    pallas_call x1, Pallas kernels, scatter_grads(): pl.pallas_call(functools.partial(scatter_kernel, grid, units, len(grads))...  89.8 us
    pallas_call x1, Pallas kernels, gather_weights(): pl.pallas_call(functools.partial(gather_kernel, grid, units, len(weights)...  83.4 us
    dot_general x21, matrix products, dot(): lax.dot_general(a, b, (contract, ((), ())), preferred_element_type=f32)  57.4 us
    pallas_call x2, Pallas kernels, exchange_states(): pl.pallas_call(functools.partial(state_kernel, grid, backward), out_shape...  49 us
    pallas_call x4, Pallas kernels, call(): pl.pallas_call(kernel, out_shape=tuple((jax.ShapeDtypeStruct(s, d) for s,...  37.2 us
    unnamed x76, local copies, waits for them, and re-layouts  13.3 us

profile of v1, /device:TPU:0, one launch (start us, length us, event | category | flops | bytes accessed | tf_op | source)
XLA Modules:
  0.0 344.2 jit_solution(11111732539021904556)
XLA Ops:
  0.7 0.6 copy-done
  1.3 0.8 fusion.16
  2.1 0.9 fusion.28
  3.0 0.9 fusion.27
  3.8 0.9 fusion.26
  4.7 0.9 fusion.25
  5.5 0.9 fusion.24
  6.4 1.3 concatenate.6.refs_6_
  7.6 83.4 %gather_weights.1 = (bf16[2,16,24,768]{3,2,1,0:T(8,128)(2,1)}, bf16[2,16,24,768]{3,2,1,0:T(8,128)(2,1)}, bf16[2,16,24,768]{3,2,1,0:T(8,128)(2,1)}, bf16[2,16,24,...) custom-call(bf16[24,768]{1,0:T(8,128)(2,1)} %refs_0_.1, ...), custom_call_target="tpu_custom_call" | custom-call | tf_op jit(solution)/shard_map/gather_weights/pallas_call | solution.py:266
  91.0 0.9 slice_reduce_fusion.1
  92.0 7.0 %projections.1 = (bf16[512,768]{1,0:T(8,128)(2,1)}, bf16[512,768]{1,0:T(8,128)(2,1)}, bf16[512,768]{1,0:T(8,128)(2,1)}, f32[512,768]{1,0:T(8,128)}, f32[512,768]...) custom-call(bf16[512,768]{1,0:T(8,128)(2,1)} %bitcast.113, bf16[768,768]{1,0:T(8,128)(2,1)} %bitcast.106, ...), custom_call_target="tpu_custom_call" | custom-call | tf_op jit(solution)/shard_map/projections/pallas_call | solution.py:748
  99.0 23.9 %exchange_states.2 = (bf16[6,128,128]{2,1,0:T(8,128)(2,1)}, f32[8,768]{1,0:T(8,128)}) custom-call(f32[6,128,128]{2,1,0:T(8,128)} %get-tuple-element.54.refs_0_, f32[8,768]{1,0:T(8,128)} %get-tuple-element.55.refs_1_), custom_call_target="tpu_custom_call" | custom-call | tf_op jit(solution)/shard_map/exchange_states/pallas_call | solution.py:515
  123.0 9.5 %attend.1 = (bf16[512,768]{1,0:T(8,128)(2,1)}, f32[512,768]{1,0:T(8,128)}) custom-call(s32[1,512]{1,0:T(1,128)} %pos.7, f32[512,768]{1,0:T(8,128)} %get-tuple-element.51.sq, f32[512,768]{1,0:T(8,128)} %get-tuple-element.52.sk, bf16[512,768]{1,0:T(8,128)(2,1)} %get-tuple-element.53.v, bf16[6,128,128]{2,1,0:T(8,128)(2,1)} %get-tuple-element.56.entering, ...), custom_call_target="tpu_custom_call" | custom-call | tf_op jit(solution)/shard_map/attend/pallas_call | solution.py:748
  132.4 2.1 fusion.58
  135.0 4.8 %fusion.54 = f32[512,3072]{1,0:T(8,128)} fusion(bf16[768,3072]{1,0:T(8,128)(2,1)S(1)} %bitcast.115, f32[512,768]{1,0:T(8,128)S(1)} %get-tuple-element.103, f32[768]{0:T(1024)S(1)} %get-tuple-element.92, f32[768]{0:T(1024)S(1)} %get-tuple-element.93, f32[512]{0:T(512)S(1)} %add_rsqrt_fusion.1, f32[512]{0:T(512)S(1)} %broadcast_multiply_fusion.5), kind=kOutput, calls=%fused_computation.102 | convolution fusion | flops 2417885184 | bytes 12593152 | tf_op jit(solution)/shard_map/dot_general | solution.py:541
  139.8 0.7 slice.38
  140.6 7.8 %fusion.59 = (f32[512]{0:T(512)S(1)}, f32[512,768]{1,0:T(8,128)S(1)}) fusion(f32[768]{0:T(1024)S(1)} %get-tuple-element.91, bf16[3072,768]{1,0:T(8,128)(2,1)} %bitcast.119, f32[512,3072]{1,0:T(8,128)} %fusion.54, f32[3072]{0:T(1024)S(1)} %add.130, f32[768]{0:T(1024)S(1)} %get-tuple-element.92, f32[768]{0:T(1024)S(1)} %get-tuple-element.93, ...), kind=kOutput, calls=%fused_computation.105 | convolution fusion | flops 2434399744 | bytes 14183424 | tf_op jit(solution)/shard_map/dot_general | solution.py:541
  148.7 0.8 copy-done.2
  149.5 0.8 fusion.15
  150.3 1.6 convert_reduce_fusion.2
  151.9 0.7 copy-done.28
  152.6 9.4 %convert_reduce_fusion = (f32[3072]{0:T(1024)}, bf16[512,3072]{1,0:T(8,128)(2,1)S(1)}) fusion(f32[512,3072]{1,0:T(8,128)S(1)} %copy-done.28, f32[3072]{0:T(1024)S(1)} %add.130, bf16[3072,768]{1,0:T(8,128)(2,1)} %bitcast.120, f32[512,768]{1,0:T(8,128)S(1)} %get-tuple-element.95), kind=kOutput, calls=%fused_computation.9 | convolution fusion | flops 2452485120 | bytes 15753216 | tf_op jit(solution)/shard_map/dot_general | solution.py:541
  162.0 3.6 %multiply_reduce_fusion = (f32[768]{0:T(1024)}, f32[512]{0:T(512)S(1)}, f32[512]{0:T(512)S(1)}, f32[768]{0:T(1024)}, f32[512,768]{1,0:T(8,128)S(1)}) fusion(f32[512,768]{1,0:T(8,128)S(1)} %get-tuple-element.103, f32[512]{0:T(512)S(1)} %add_rsqrt_fusion.1, f32[512]{0:T(512)S(1)} %broadcast_multiply_fusion.5, f32[768]{0:T(1024)S(1)} %get-tuple-element.93, ...), kind=kOutput, calls=%fused_computation.24 | convolution fusion | flops 2419848704 | bytes 12600320 | tf_op jit(solution)/shard_map/dot_general | solution.py:541
  166.1 0.8 copy-done.25
  166.9 1.7 convolution_convert_fusion.6.grad_mixed
  168.7 6.1 %use.1 = (bf16[512,768]{1,0:T(8,128)(2,1)}, f32[512,768]{1,0:T(8,128)}, f32[6,128,128]{2,1,0:T(8,128)}, f32[8,768]{1,0:T(8,128)}) custom-call(s32[1,512]{1,0:T(1,128)} %pos.7, f32[512,768]{1,0:T(8,128)} %get-tuple-element.51.sq, bf16[512,768]{1,0:T(8,128)(2,1)} %get-tuple-element.58.mixed, f32[512,768]{1,0:T(8,128)} %get-tuple-element.65.inverse, ...), custom_call_target="tpu_custom_call" | custom-call | tf_op jit(solution)/shard_map/use/pallas_call | solution.py:748
  174.7 25.1 %exchange_states.3 = (bf16[6,128,128]{2,1,0:T(8,128)(2,1)}, f32[8,768]{1,0:T(8,128)}) custom-call(f32[6,128,128]{2,1,0:T(8,128)} %get-tuple-element.68.refs_0_, f32[8,768]{1,0:T(8,128)} %get-tuple-element.69.refs_1_), custom_call_target="tpu_custom_call" | custom-call | tf_op jit(solution)/shard_map/exchange_states/pallas_call | solution.py:515
  199.8 14.7 %back.1 = (bf16[512,768]{1,0:T(8,128)(2,1)}, bf16[512,768]{1,0:T(8,128)(2,1)}, bf16[512,768]{1,0:T(8,128)(2,1)}) custom-call(s32[1,512]{1,0:T(1,128)} %pos.7, bf16[512,768]{1,0:T(8,128)(2,1)} %get-tuple-element.63.q, bf16[512,768]{1,0:T(8,128)(2,1)} %get-tuple-element.64.k, bf16[512,768]{1,0:T(8,128)(2,1)} %get-tuple-element.53.v, ...), custom_call_target="tpu_custom_call" | custom-call | tf_op jit(solution)/shard_map/back/pallas_call | solution.py:748
  214.6 2.1 fusion.61
  216.7 0.8 fusion.60
  218.2 2.0 add_bitcast_fusion
  220.2 1.9 convolution_convert_fusion.5
  222.1 1.9 convolution_convert_fusion.4
  224.0 1.9 convolution_convert_fusion.3
  225.8 1.8 convolution_convert_fusion.2
  227.7 4.9 %convolution_convert_fusion.1 = bf16[768,3072]{1,0:T(8,128)(2,1)} fusion(bf16[512,3072]{1,0:T(8,128)(2,1)S(1)} %copy-done.30, f32[512,768]{1,0:T(8,128)S(1)} %get-tuple-element.103, f32[768]{0:T(1024)S(1)} %copy-done.20, f32[768]{0:T(1024)S(1)} %get-tuple-element.93, f32[512]{0:T(512)S(1)} %copy-done.18, f32[512]{0:T(512)S(1)} %broadcast_multiply_fusion.5), kind=kOutput, calls=%fused_computation.12 | convolution fusion | flops 2420244480 | bytes 9447424 | tf_op jit(solution)/shard_map/dot_general | solution.py:541
  232.7 5.5 %convolution_convert_fusion = bf16[3072,768]{1,0:T(8,128)(2,1)} fusion(f32[512,768]{1,0:T(8,128)S(1)} %copy-done.6, f32[512,3072]{1,0:T(8,128)S(1)} %bitcast.124, f32[3072]{0:T(1024)S(1)} %copy-done.15), kind=kOutput, calls=%fused_computation.11 | convolution fusion | flops 2434400256 | bytes 12595200 | tf_op jit(solution)/shard_map/dot_general | solution.py:541
  238.5 1.3 concatenate.7.refs_6_
  239.7 89.8 %scatter_grads.1 = (f32[24,768]{1,0:T(8,128)}, f32[24,768]{1,0:T(8,128)}, f32[24,768]{1,0:T(8,128)}, f32[24,768]{1,0:T(8,128)}, f32[24,3072]{1,0:T(8,128)}, /*index=5*/f32[96,768]{1,0:T(8,128)}, f32[16,768]{1,0:T(8,128)}) custom-call(bf16[2,16,24,768]{3,2,1,0:T(8,128)(2,1)} %bitcast.110, bf16[2,16,24,768]{3,2,1,0:T(8,128)(2,1)} %bitcast.111, ...), custom_call_target="tpu_custom_call" | custom-call | tf_op jit(solution)/shard_map/scatter_grads/pallas_call | solution.py:402
  329.6 0.7 slice.42
  330.9 0.9 fusion.57
  331.8 0.6 fusion.34
  334.7 1.5 copy.38
  336.3 1.5 copy.39
  337.8 1.5 copy.40
  339.3 1.5 copy.41
  340.8 1.7 copy.42
  342.5 1.7 copy.43
  (97 shorter events, 5.1 us)
Async XLA Ops:
  0.6 0.7 copy-start
  6.4 92.6 %copy-start.12 = (f32[7,768]{1,0:T(8,128)}, f32[7,768]{1,0:T(8,128)S(1)}, u32[]{:S(2)}) copy-start(f32[7,768]{1,0:T(8,128)S(1)} %broadcast.97) | copy-start | bytes 64516
  92.0 48.6 %copy-start.19 = (f32[768]{0:T(1024)}, f32[768]{0:T(1024)S(1)}, u32[]{:S(2)}) copy-start(f32[768]{0:T(1024)S(1)} %get-tuple-element.92) | copy-start | bytes 9220
  122.9 9.5 %copy-start.9 = (bf16[1,512,768]{2,1,0:T(8,128)(2,1)S(1)}, bf16[1,512,768]{2,1,0:T(8,128)(2,1)}, u32[]{:S(2)}) copy-start(bf16[1,512,768]{2,1,0:T(8,128)(2,1)} %param.15) | copy-start | bytes 2359300
  123.0 9.5 %copy-start.24 = (bf16[2,16,24,768]{3,2,1,0:T(8,128)(2,1)S(1)}, bf16[2,16,24,768]{3,2,1,0:T(8,128)(2,1)}, u32[]{:S(2)}) copy-start(bf16[2,16,24,768]{3,2,1,0:T(8,128)(2,1)} %get-tuple-element.59) | copy-start | bytes 3538948
  132.4 2.6 copy-start.23
  135.0 30.7 %copy-start.17 = (f32[512]{0:T(512)}, f32[512]{0:T(512)S(1)}, u32[]{:S(2)}) copy-start(f32[512]{0:T(512)S(1)} %add_rsqrt_fusion.1) | copy-start | bytes 6148
  140.6 11.3 %copy-start.14 = (f32[3072]{0:T(1024)}, f32[3072]{0:T(1024)S(1)}, u32[]{:S(2)}) copy-start(f32[3072]{0:T(1024)S(1)} %add.130) | copy-start | bytes 36868
  148.4 1.1 copy-start.2
  149.5 3.1 copy-start.28
  150.3 11.7 %slice-start = ((s8[4718592]{0:T(1024)(128)(4,1)}), s8[4194304]{0:T(1024)(128)(4,1)S(1)}, s32[]{:S(2)}) async-start(s8[4718592]{0:T(1024)(128)(4,1)} %bitcast.116), calls=%async_computation | async-start | bytes 8388608
  151.9 10.1 %copy-start.5 = (f32[512,768]{1,0:T(8,128)}, f32[512,768]{1,0:T(8,128)S(1)}, u32[]{:S(2)}) copy-start(f32[512,768]{1,0:T(8,128)S(1)} %get-tuple-element.95) | copy-start | bytes 4718596
  152.6 9.4 %slice-start.1 = ((s8[4718592]{0:T(1024)(128)(4,1)}), s8[524288]{0:T(1024)(128)(4,1)S(1)}, s32[]{:S(2)}) async-start(s8[4718592]{0:T(1024)(128)(4,1)} %bitcast.116), calls=%async_computation.1 | async-start | bytes 1048576
  162.0 3.6 %copy-start.29 = (bf16[512,3072]{1,0:T(8,128)(2,1)}, bf16[512,3072]{1,0:T(8,128)(2,1)S(1)}, u32[]{:S(2)}) copy-start(bf16[512,3072]{1,0:T(8,128)(2,1)S(1)} %get-tuple-element.108) | copy-start | bytes 9437188
  165.7 1.3 copy-start.25
  199.8 14.7 %copy-start.8 = (bf16[2,16,24,768]{3,2,1,0:T(8,128)(2,1)S(1)}, bf16[2,16,24,768]{3,2,1,0:T(8,128)(2,1)}, u32[]{:S(2)}) copy-start(bf16[2,16,24,768]{3,2,1,0:T(8,128)(2,1)} %get-tuple-element.49) | copy-start | bytes 3538948
  214.6 2.1 copy-start.7
  214.6 2.1 copy-start.27
  216.7 1.3 copy-start.3
  216.7 1.5 copy-start.11
  218.2 2.0 copy-start.10
  220.2 1.9 copy-start.26
  223.9 1.9 copy-start.4
  224.0 3.7 %copy-start.30 = (bf16[512,3072]{1,0:T(8,128)(2,1)S(1)}, bf16[512,3072]{1,0:T(8,128)(2,1)}, u32[]{:S(2)}) copy-start(bf16[512,3072]{1,0:T(8,128)(2,1)} %copy-done.29) | copy-start | bytes 9437188
  225.8 1.8 copy-start.18
  225.8 1.8 copy-start.20
  225.8 6.8 %slice-start.2 = ((s8[6291456]{0:T(1024)(128)(4,1)}), s8[4194304]{0:T(1024)(128)(4,1)S(1)}, s32[]{:S(2)}) async-start(s8[6291456]{0:T(1024)(128)(4,1)} %bitcast.123), calls=%async_computation.2 | async-start | bytes 8388608
  227.7 5.0 %copy-start.6 = (f32[512,768]{1,0:T(8,128)S(1)}, f32[512,768]{1,0:T(8,128)}, u32[]{:S(2)}) copy-start(f32[512,768]{1,0:T(8,128)} %copy-done.5) | copy-start | bytes 4718596
  227.7 5.0 %copy-start.15 = (f32[3072]{0:T(1024)S(1)}, f32[3072]{0:T(1024)}, u32[]{:S(2)}) copy-start(f32[3072]{0:T(1024)} %copy-done.14) | copy-start | bytes 36868
  227.7 5.0 %slice-start.3 = ((s8[6291456]{0:T(1024)(128)(4,1)}), s8[2097152]{0:T(1024)(128)(4,1)S(1)}, s32[]{:S(2)}) async-start(s8[6291456]{0:T(1024)(128)(4,1)} %bitcast.123), calls=%async_computation.3 | async-start | bytes 4194304
  232.7 5.6 %copy-start.16 = (f32[3072]{0:T(1024)S(1)}, f32[3072]{0:T(1024)}, u32[]{:S(2)}) copy-start(f32[3072]{0:T(1024)} %get-tuple-element.107) | copy-start | bytes 36868
  232.7 5.6 %copy-start.22 = (f32[768]{0:T(1024)S(1)}, f32[768]{0:T(1024)}, u32[]{:S(2)}) copy-start(f32[768]{0:T(1024)} %get-tuple-element.82) | copy-start | bytes 9220
  232.7 5.6 %copy-start.21 = (f32[768]{0:T(1024)S(1)}, f32[768]{0:T(1024)}, u32[]{:S(2)}) copy-start(f32[768]{0:T(1024)} %get-tuple-element.87) | copy-start | bytes 9220
  232.7 5.8 %copy-start.13 = (f32[7,768]{1,0:T(8,128)S(1)}, f32[7,768]{1,0:T(8,128)}, u32[]{:S(2)}) copy-start(f32[7,768]{1,0:T(8,128)} %copy-done.12) | copy-start | bytes 64516
  239.7 104.5 %copy-start.1 = (bf16[96]{0:T(256)(128)(2,1)S(1)}, bf16[96]{0:T(256)(128)(2,1)}, u32[]{:S(2)}) copy-start(bf16[96]{0:T(256)(128)(2,1)} %param.22) | copy-start | bytes 580
